TPU v7x, 256 devices: a whole 4x4x8 slice. The times are simulated.
256 devices in a mesh: chan: 64 (over z_hi, x, y, core), tm: 4 (over z_lo).
Axes of the slice: x: 4, y: 4, z: 8 (z_hi: 2, z_lo: 4; z = z_hi * 4 + z_lo), core: 2. Of those that a mesh axis runs over, the one named last changes fastest.
Arguments:
- spectra: bfloat16 [64, 8, 2, 6144], P(None, 'tm', None, 'chan'), may hold values from -120 to 120
- bad_channels: int32 [6144], P('chan'), may hold values 0 or 1
- tile_list: int32 [512, 2], P('chan'), may hold values from 0 to 47, as said below
Outputs:
- correlations: float32 [512, 32, 128, 128], P(('chan', 'tm'))
Inputs may be any that keep to these rules, and one draw needn't show every extreme that they name: `tile_list`: each row (a, b) has a <= b; a pair may appear more than once.
All inputs are finite; a program needn't handle non-finite values. No bound on the sum of `bad_channels` on one device may be relied on, other than what follows from the above.
Results may differ from a plain program's by a relative error of at most 0.004.
Values may be sent and summed in bfloat16 or wider, within the bound.
A program may use at most 128 MiB of HBM per device.

v0:
```python
import math

import jax
import jax.numpy as jnp
from jax import lax
from jax.sharding import PartitionSpec as P

HR_DEV = 2
F = 64
LAGS = 32
TILE = 128


EPSILON = 1e-06


def whiten(spectra, bad_channels):
    values = spectra.astype(jnp.float32)
    power = jnp.mean(values * values, axis=(0, 2))
    keep_mask = (1 - bad_channels).astype(jnp.float32)
    white = values * lax.rsqrt(power + EPSILON)[None, :, None, :] * keep_mask[None, None, None, :]
    return white.astype(jnp.bfloat16)


def lag_table(hour_count):
    bin_number = jnp.arange(F, dtype=jnp.float32) + 1.0
    lag_steps = jnp.arange(LAGS, dtype=jnp.float32) - float(LAGS // 2)
    phases = math.pi / F * bin_number[:, None] * lag_steps[None, :]
    norm_scale = 1.0 / math.sqrt(F * hour_count)
    return jnp.stack([jnp.cos(phases) * norm_scale, -jnp.sin(phases) * norm_scale], axis=1)


def take_block(spectra_all, block_index):
    return lax.dynamic_slice_in_dim(spectra_all, block_index * TILE, TILE, axis=3)


def cross_spec(spectra_all, tile_pair):
    left_block = take_block(spectra_all, tile_pair[0])
    right_block = take_block(spectra_all, tile_pair[1])
    bin_total = left_block.shape[0]
    hour_count = left_block.shape[1]
    row_block = left_block.reshape(bin_total, 2 * hour_count, TILE)
    turned = jnp.stack([-right_block[:, :, 1], right_block[:, :, 0]], axis=2)
    col_block = jnp.concatenate([right_block, turned], axis=3).reshape(
        bin_total, 2 * hour_count, 2 * TILE
    )
    return jnp.einsum("fki,fkj->fij", row_block, col_block, preferred_element_type=jnp.float32)


def transform(cross, table):
    parted = cross.reshape(cross.shape[0], TILE, 2, TILE)
    return jnp.einsum("fixj,fxt->tij", parted, table, precision=lax.Precision.HIGHEST)


def tile_lags(spectra_all, table, pairs):
    return jax.vmap(lambda tile_pair: transform(cross_spec(spectra_all, tile_pair), table))(pairs)


def per_device(spectra, bad_channels, tile_list):
    white = whiten(spectra, bad_channels)
    tile_dev = tile_list.shape[0] // lax.axis_size("tm")
    table = lag_table(HR_DEV * lax.axis_size("tm"))
    hours_all = lax.all_gather(white, "tm", axis=1, tiled=True)
    spectra_all = lax.all_gather(hours_all, "chan", axis=3, tiled=True)
    own_pairs = lax.dynamic_slice_in_dim(
        tile_list, lax.axis_index("tm") * tile_dev, tile_dev, axis=0
    )
    return tile_lags(spectra_all, table, own_pairs)


def solution(mesh):
    placed = (P(None, "tm", None, "chan"), P("chan"), P("chan", None))
    return jax.shard_map(
        per_device,
        mesh=mesh,
        in_specs=placed,
        out_specs=P(("chan", "tm"), None, None, None),
        check_vma=False,
    )
```

profile of v0, /device:TPU:1, one launch (start us, length us, event | category | flops | bytes accessed | tf_op | source)
XLA Modules:
  0.0 306.1 jit_solution(9711034003275333782)
XLA Ops:
  6.5 0.0 copy-start
  6.5 0.0 all-gather.2.cloned.1.call-start
  6.5 0.9 fusion.7
  7.4 0.7 subtract_convert_fusion
  8.1 0.9 fusion.9
  9.0 13.7 %all_gather.6 = bf16[64,8,2,96]{3,0,2,1:T(8,128)(2,1)S(1)} all-gather(bf16[64,2,2,96]{3,0,2,1:T(8,128)(2,1)S(1)} %fusion.9), channel_id=1, replica_groups=mesh['chan'=64,'tm'=4] {'tm'}, dimensions={1}, use_global_device_ids=true | all-gather | bytes 245760 | tf_op jit(solution)/shard_map/all_gather | solution.py:63
  22.7 1.1 copy.15
  23.7 0.0 all-gather.2.cloned.1.call-update
  23.8 0.0 copy-done
  23.8 0.1 constant_dynamic-slice_fusion
  23.9 0.1 fusion.12
  24.0 204.5 %all-gather.2.cloned.1.call-done = bf16[64,8,2,6144]{0,1,2,3:T(8,128)(2,1)} async-done(((bf16[64,8,2,96]{0,1,2,3:T(8,128)(2,1)}), bf16[64,8,2,6144]{0,1,2,3:T(8,128)(2,1)}) %all-gather.2.cloned.1.call-update) | async-done | bytes 12582928 | tf_op jit(solution)/shard_map/all_gather | solution.py:64
  228.5 8.9 %gather_fusion.1 = bf16[2,64,8,2,128]{1,2,3,4,0:T(8,128)(2,1)S(1)} fusion(bf16[64,8,2,6144]{0,1,2,3:T(8,128)(2,1)} %all-gather.2.cloned.1.call-done, s32[2]{0:T(128)S(1)} %get-tuple-element.10), kind=kCustom, calls=%fused_computation.1 | custom fusion | bytes 1048608 | tf_op jit(solution)/shard_map/vmap()/gather | solution.py:34
  237.4 0.1 slice_negate_fusion
  237.6 0.5 maximum_maximum_fusion
  238.1 3.1 %copy.17 = bf16[2,64,8,2,256]{4,3,2,1,0:T(2,128)(2,1)S(1)} copy(bf16[2,64,8,2,256]{1,2,3,4,0:T(8,128)(2,1)S(1)} %maximum_maximum_fusion) | data formatting | bytes 2097152 | tf_op jit(solution)/shard_map/vmap()/concatenate | solution.py:44
  241.2 0.4 reshape.116
  241.6 8.9 %gather_fusion = bf16[2,64,8,2,128]{1,2,3,4,0:T(8,128)(2,1)S(1)} fusion(bf16[64,8,2,6144]{0,1,2,3:T(8,128)(2,1)} %all-gather.2.cloned.1.call-done, s32[2]{0:T(128)S(1)} %get-tuple-element.9), kind=kCustom, calls=%fused_computation | custom fusion | bytes 1048608 | tf_op jit(solution)/shard_map/vmap()/gather | solution.py:34
  250.5 0.9 copy.16
  251.4 8.1 %fusion.5 = f32[2,64,128,256]{3,2,1,0:T(8,128)} fusion(bf16[2,64,16,256]{3,2,1,0:T(8,128)(2,1)S(1)} %reshape.116, bf16[2,64,16,128]{3,1,2,0:T(8,128)(2,1)S(1)} %bitcast.18), kind=kOutput, calls=%fused_computation.7 | convolution fusion | flops 134217728 | bytes 18350080 | tf_op jit(solution)/shard_map/vmap(fki,fkj->fij)/dot_general | solution.py:47
  259.5 0.0 copy-start.1
  259.5 20.8 %reshape.117 = f32[2,64,128,2,128]{4,3,2,1,0:T(2,128)} reshape(f32[2,64,128,256]{3,2,1,0:T(8,128)} %fusion.5) | data formatting | bytes 33554432 | tf_op jit(solution)/shard_map/vmap()/reshape | solution.py:51
  280.3 14.5 %fusion.2 = f32[2,32,128,128]{3,1,2,0:T(8,128)S(1)} fusion(f32[2,64,128,2,128]{4,3,2,1,0:T(2,128)} %reshape.117, f32[64,1,32]{0,2,1:T(8,128)S(1)} %get-tuple-element.8, f32[64,1,32]{0,2,1:T(8,128)S(1)} %get-tuple-element.7), kind=kOutput, calls=%fused_computation.4 | convolution fusion | flops 1610616832 | bytes 20987904 | tf_op jit(solution)/shard_map/vmap(fixj,fxt->tij)/dot_general | solution.py:52
  294.8 4.4 %copy.20 = f32[2,32,128,128]{3,2,1,0:T(8,128)} copy(f32[2,32,128,128]{3,1,2,0:T(8,128)S(1)} %fusion.2) | data formatting | bytes 8388608 | tf_op jit(solution)/shard_map/vmap()/transpose | solution.py:56
  299.2 0.0 copy-done.1
  (4 shorter events, 0.0 us)
Async XLA Ops:
  6.5 17.3 %copy-start = (s32[8,2]{0,1:T(2,128)S(1)}, s32[8,2]{0,1:T(2,128)}, u32[]{:S(2)}) copy-start(s32[8,2]{0,1:T(2,128)} %param.5) | copy-start | bytes 196
  6.5 222.0 %all-gather.2.cloned.1.call-start = ((), (), s32[]{:S(2)}) async-start(), calls=%async_computation | async-start | bytes 25559040 | tf_op jit(solution)/shard_map/all_gather | solution.py:64
  259.5 39.7 %copy-start.1 = (s32[8,2]{0,1:T(2,128)S(1)}, s32[8,2]{0,1:T(2,128)}, u32[]{:S(2)}) copy-start(s32[8,2]{0,1:T(2,128)} %param.5) | copy-start | bytes 196
Sparse Core Ops, SparseCore 0:
  23.9 204.5 all-gather.1
where the time goes:
time: 307 us; the launch traced here: 306 us
  waiting for transfers between devices  205 us (67%)
  local copies, waits for them, and re-layouts  48.6 us (16%)
  matrix products  22.6 us (7%)
  blocking collectives  13.7 us (4%)
  between operations  13.5 us (4%)
  other arithmetic  3.19 us (1%)
    all_gather x1, waiting for transfers between devices, per_device(): spectra_all = lax.all_gather(hours_all, 'chan', axis=3, tiled=True)  204 us
    reshape x1, local copies, waits for them, and re-layouts, transform(): parted = cross.reshape(cross.shape[0], TILE, 2, TILE)  20.8 us
    gather x3, local copies, waits for them, and re-layouts, take_block(): lax.dynamic_slice_in_dim(spectra_all, block_index * TILE, TILE, axis=3)  18.7 us
    dot_general x1, matrix products, transform(): jnp.einsum('fixj,fxt->tij', parted, table, precision=lax.Precision.HIGHEST)  14.5 us
    all_gather x1, blocking collectives, per_device(): hours_all = lax.all_gather(white, 'tm', axis=1, tiled=True)  13.7 us
    dot_general x1, matrix products, cross_spec(): jnp.einsum('fki,fkj->fij', row_block, col_block, preferred_element_type=j...  8.11 us
  transfers between devices with their start and end apart: 1, of which 1 were waited for; matrix products, arithmetic and copies ran while one was open for 0% of the time, Pallas kernels for 0%

commit v1 on v0

v1 whole, which is shorter than its diff:
```python
import functools
import math

import jax
import jax.numpy as jnp
import numpy as np
from jax import lax
from jax.experimental import pallas as pl
from jax.experimental.pallas import tpu as pltpu
from jax.sharding import PartitionSpec as P

F = 64
HOURS = 8
LAGS = 32
TILE = 128
CHANNELS = 6144
EPSILON = 1e-06

PLANE = 32
SHARD = 96
HALF_BLOCKS = 24
ROWS = 8
SLOTS = 4
MESH_ID = pl.DeviceIdType.MESH
CHUNK_OF_STEP = ((2, 0), (6, 0), (7, 1), (3, 1), (1, 2), (5, 2), (4, 3))


def exchange_kernel(
    spec_ref, bad_ref, tile_ref, out_ref,
    white, mine, tiles_in, tiles, zb0, zb1, zb2, zb3, pack,
    sem_a_send, sem_a_recv, sem_t_send, sem_t_recv, sem_t_local, sem_z_send, sem_z_recv, sem_p_send, sem_p_recv,
):
    zbs = (zb0, zb1, zb2, zb3)
    chan, tm = lax.axis_index("chan"), lax.axis_index("tm")
    half = chan // PLANE
    me = chan % PLANE
    x, y, core = me // 8, (me // 2) % 4, me % 2
    z = half * 4 + tm

    def plane_peer(j):
        dx, dy, dc = j // 8, (j // 2) % 4, j % 2
        k = ((x + dx) % 4) * 8 + ((y + dy) % 4) * 2 + (core + dc) % 2
        return k, (half * PLANE + k, tm)

    def z_peer(step):
        zz = (z + step) % 8
        return ((zz // 4) * PLANE + me, zz % 4)

    barrier = pltpu.get_barrier_semaphore()

    def greet(j, carry):
        _, dev = plane_peer(j)
        pl.semaphore_signal(barrier, inc=1, device_id=dev, device_id_type=MESH_ID)
        return carry

    lax.fori_loop(1, PLANE, greet, 0)
    for step, _ in CHUNK_OF_STEP:
        pl.semaphore_signal(barrier, inc=1, device_id=z_peer(step), device_id_type=MESH_ID)

    values = spec_ref[...].astype(jnp.float32)
    squares = jnp.sum((values * values).reshape(F // 2, ROWS, SHARD), axis=0)
    row = lax.broadcasted_iota(jnp.int32, (ROWS, SHARD), 0)
    first = (row % 4) < 2
    power0 = jnp.sum(jnp.where(first, squares, 0.0), axis=0, keepdims=True) / (2 * F)
    power1 = jnp.sum(jnp.where(first, 0.0, squares), axis=0, keepdims=True) / (2 * F)
    scale = lax.rsqrt(jnp.where(first, power0, power1) + EPSILON)
    keep = (1 - bad_ref[...]).astype(jnp.float32)
    whitened = values.reshape(F // 2, ROWS, SHARD) * scale[None] * keep[None]
    padded = jnp.concatenate([whitened, jnp.zeros((F // 2, ROWS, TILE - SHARD), jnp.float32)], axis=2)
    white[...] = padded.astype(jnp.bfloat16)

    pl.semaphore_wait(barrier, PLANE - 1 + 7)

    own_tiles = pltpu.make_async_copy(tile_ref, tiles_in.at[me], sem_t_recv)
    own_tiles.start()
    own_slice = pltpu.make_async_copy(white.at[me], mine.at[me], sem_a_recv)
    own_slice.start()

    def spread(j, carry):
        k, dev = plane_peer(j)
        pltpu.make_async_remote_copy(
            src_ref=white.at[k], dst_ref=mine.at[me], send_sem=sem_a_send, recv_sem=sem_a_recv,
            device_id=dev, device_id_type=MESH_ID,
        ).start()
        return carry

    lax.fori_loop(1, PLANE, spread, 0)

    def spread_tiles(j, carry):
        _, dev = plane_peer(j)
        pltpu.make_async_remote_copy(
            src_ref=tile_ref, dst_ref=tiles_in.at[me], send_sem=sem_t_send, recv_sem=sem_t_recv,
            device_id=dev, device_id_type=MESH_ID,
        ).start()
        return carry

    lax.fori_loop(1, PLANE, spread_tiles, 0)

    pltpu.make_async_copy(mine, mine, sem_a_recv).wait()

    lane = lax.broadcasted_iota(jnp.int32, (ROWS, TILE), 1)
    base = half * HALF_BLOCKS
    for g in range(PLANE // 4):
        s0, s1, s2, s3 = (mine[4 * g + i].astype(jnp.float32) for i in range(4))
        s1 = pltpu.roll(s1, 96, 1)
        s2 = pltpu.roll(s2, 64, 1)
        s3 = pltpu.roll(s3, 32, 1)
        zb3[base + 3 * g] = jnp.where(lane < 96, s0, s1).astype(jnp.bfloat16)
        zb3[base + 3 * g + 1] = jnp.where(lane < 64, s1, s2).astype(jnp.bfloat16)
        zb3[base + 3 * g + 2] = jnp.where(lane < 32, s2, s3).astype(jnp.bfloat16)

    for step, chunk in CHUNK_OF_STEP:
        pltpu.make_async_remote_copy(
            src_ref=zb3.at[pl.ds(base, HALF_BLOCKS)], dst_ref=zbs[chunk].at[pl.ds(base, HALF_BLOCKS)],
            send_sem=sem_z_send, recv_sem=sem_z_recv.at[chunk],
            device_id=z_peer(step), device_id_type=MESH_ID,
        ).start()

    pltpu.make_async_copy(tiles_in, tiles_in, sem_t_recv).wait()
    to_smem = pltpu.make_async_copy(tiles_in, tiles, sem_t_local)
    to_smem.start()
    to_smem.wait()

    for chunk in range(4):
        t = (tm + (2, 1, 3, 0)[chunk]) % 4
        zb = zbs[chunk]
        if chunk < 3:
            pltpu.make_async_copy(zb, zb, sem_z_recv.at[chunk]).wait()
        else:
            other = zb.at[pl.ds((1 - half) * HALF_BLOCKS, HALF_BLOCKS)]
            pltpu.make_async_copy(other, other, sem_z_recv.at[chunk]).wait()

        def select(j, carry):
            k, _ = plane_peer(j)
            for s in range(SLOTS):
                pack[chunk, k, s] = zb[tiles[k, 0, SLOTS * tm + s]]
            return carry

        lax.fori_loop(0, PLANE, select, 0)
        pltpu.make_async_copy(pack.at[chunk, me], out_ref.at[t, me], sem_p_recv).start()

        def deliver(j, carry):
            k, dev = plane_peer(j)
            pltpu.make_async_remote_copy(
                src_ref=pack.at[chunk, k], dst_ref=out_ref.at[t, me], send_sem=sem_p_send, recv_sem=sem_p_recv,
                device_id=dev, device_id_type=MESH_ID,
            ).start()
            return carry

        lax.fori_loop(1, PLANE, deliver, 0)

    pltpu.make_async_copy(out_ref, out_ref, sem_p_recv).wait()
    sent = white.at[pl.ds(0, PLANE - 1)]
    pltpu.make_async_copy(sent, sent, sem_a_send).wait()
    sent = tiles_in.at[pl.ds(0, PLANE - 1)]
    pltpu.make_async_copy(sent, sent, sem_t_send).wait()
    for _ in CHUNK_OF_STEP:
        sent = zb3.at[pl.ds(0, HALF_BLOCKS)]
        pltpu.make_async_copy(sent, sent, sem_z_send).wait()
    sent = pack.at[:, pl.ds(0, PLANE - 1)]
    pltpu.make_async_copy(sent, sent, sem_p_send).wait()


def exchange(spectra, bad, tile_row):
    vmem = pl.BlockSpec(memory_space=pltpu.VMEM)
    slab = pltpu.VMEM((2 * HALF_BLOCKS, ROWS, TILE), jnp.bfloat16)
    return pl.pallas_call(
        exchange_kernel,
        out_shape=jax.ShapeDtypeStruct((4, PLANE, SLOTS, ROWS, TILE), jnp.bfloat16),
        in_specs=[vmem, vmem, vmem],
        out_specs=pl.BlockSpec(memory_space=pl.ANY),
        scratch_shapes=[
            pltpu.VMEM((PLANE, ROWS, TILE), jnp.bfloat16),
            pltpu.VMEM((PLANE, ROWS, TILE), jnp.bfloat16),
            pltpu.VMEM((PLANE, 1, TILE), jnp.int32),
            pltpu.SMEM((PLANE, 1, TILE), jnp.int32),
            slab, slab, slab, slab,
            pltpu.VMEM((4, PLANE, SLOTS, ROWS, TILE), jnp.bfloat16),
            pltpu.SemaphoreType.DMA, pltpu.SemaphoreType.DMA,
            pltpu.SemaphoreType.DMA, pltpu.SemaphoreType.DMA, pltpu.SemaphoreType.DMA,
            pltpu.SemaphoreType.DMA, pltpu.SemaphoreType.DMA((4,)),
            pltpu.SemaphoreType.DMA, pltpu.SemaphoreType.DMA,
        ],
        compiler_params=pltpu.CompilerParams(collective_id=0, has_side_effects=True),
        name="exchange",
    )(spectra, bad, tile_row)


def lag_tables():
    row = np.arange(F * HOURS * 2)
    bin_number = 2 * ((row // ROWS) % PLANE) + (row % ROWS) // 4 + 1.0
    phase = np.pi / F * bin_number[None, :] * np.arange(17)[:, None]
    norm = 1.0 / math.sqrt(F * HOURS)
    return np.stack([np.cos(phase) * norm, np.sin(phase) * norm], axis=1).astype(np.float32)


def correlate_kernel(blocks_ref, table_ref, out_ref, left, right, turned):
    rows = F * HOURS * 2
    a = blocks_ref[:, :, 0].astype(jnp.float32).reshape(rows, TILE)
    left[...] = a.T
    b = blocks_ref[:, :, 1].astype(jnp.float32).reshape(rows, TILE)
    right[...] = b.astype(jnp.bfloat16)
    part = lax.broadcasted_iota(jnp.int32, (rows, TILE), 0) % 2
    turned[...] = jnp.where(part == 0, -pltpu.roll(b, rows - 1, 0), pltpu.roll(b, 1, 0)).astype(jnp.bfloat16)
    for m in range(17):
        cosines = (left[...] * table_ref[m, 0:1]).astype(jnp.bfloat16)
        c = jnp.dot(cosines, right[...], preferred_element_type=jnp.float32)
        if m == 0:
            out_ref[0, LAGS // 2] = c
            continue
        sines = (left[...] * table_ref[m, 1:2]).astype(jnp.bfloat16)
        d = jnp.dot(sines, turned[...], preferred_element_type=jnp.float32)
        if m < LAGS // 2:
            out_ref[0, LAGS // 2 + m] = c - d
        out_ref[0, LAGS // 2 - m] = c + d


def correlate(blocks, table):
    rows = F * HOURS * 2
    return pl.pallas_call(
        correlate_kernel,
        grid=(2,),
        out_shape=jax.ShapeDtypeStruct((2, LAGS, TILE, TILE), jnp.float32),
        in_specs=[
            pl.BlockSpec((4, PLANE, 2, ROWS, TILE), lambda i: (0, 0, i, 0, 0)),
            pl.BlockSpec((17, 2, rows), lambda i: (0, 0, 0)),
        ],
        out_specs=pl.BlockSpec((1, LAGS, TILE, TILE), lambda i: (i, 0, 0, 0)),
        scratch_shapes=[
            pltpu.VMEM((TILE, rows), jnp.float32),
            pltpu.VMEM((rows, TILE), jnp.bfloat16),
            pltpu.VMEM((rows, TILE), jnp.bfloat16),
        ],
        name="correlate",
    )(blocks, table)


def per_device(spectra, bad_channels, tile_list):
    rows = spectra.reshape(F * 2 * 2, SHARD)
    tile_row = jnp.pad(tile_list.reshape(1, 16), ((0, 0), (0, TILE - 16)))
    blocks = exchange(rows, bad_channels.reshape(1, SHARD), tile_row)
    return correlate(blocks, jnp.asarray(lag_tables()))


def solution(mesh):
    placed = (P(None, "tm", None, "chan"), P("chan"), P("chan", None))
    return jax.shard_map(
        per_device,
        mesh=mesh,
        in_specs=placed,
        out_specs=P(("chan", "tm"), None, None, None),
        check_vma=False,
    )
```

time: 307 us -> 47.7 us (0.16)
  waiting for transfers between devices: 205 us -> 0 us
  local copies, waits for them, and re-layouts: 48.6 us -> 1.35 us
  Pallas kernels: 0 us -> 46.2 us
  matrix products: 22.6 us -> 0 us
  blocking collectives: 13.7 us -> 0 us
  between operations: 13.5 us -> 0.01 us
  other arithmetic: 3.19 us -> 0 us
    all_gather x1 -> x0, waiting for transfers between devices: 204 us -> none  [per_device(): spectra_all = lax.all_gather(hours_all, 'chan', axis=3, tiled=True)]
    pallas_call x0 -> x2, Pallas kernels: none -> 46.2 us  [the longest x1 38.4 us: exchange(): pl.pallas_call(exchange_kernel, out_shape=jax.ShapeDtypeStruct((4, PLANE,...]
    dot_general x2 -> x0, matrix products: 22.6 us -> none  [the longest x1 14.5 us: transform(): jnp.einsum('fixj,fxt->tij', parted, table, precision=lax.Precision.HIGHEST)]
    reshape x2 -> x1, local copies, waits for them, and re-layouts: 21.2 us -> 0.08 us  [per_device(): tile_row = jnp.pad(tile_list.reshape(1, 16), ((0, 0), (0, TILE - 16)))]
    gather x3 -> x0, local copies, waits for them, and re-layouts: 18.7 us -> none  [take_block(): lax.dynamic_slice_in_dim(spectra_all, block_index * TILE, TILE, axis=3)]
    all_gather x1 -> x0, blocking collectives: 13.7 us -> none  [per_device(): hours_all = lax.all_gather(white, 'tm', axis=1, tiled=True)]
    transpose x1 -> x0, local copies, waits for them, and re-layouts: 4.44 us -> none  [tile_lags(): jax.vmap(lambda tile_pair: transform(cross_spec(spectra_all, tile_pair),...]
    concatenate x1 -> x0, local copies, waits for them, and re-layouts: 3.11 us -> none  [cross_spec(): jnp.concatenate([right_block, turned], axis=3)]
  transfers between devices with their start and end apart: 1 -> 0, of which waited for: 1 -> 0; matrix products, arithmetic and copies ran while one was open for 0% -> 0% of each run, Pallas kernels for 0% -> 0%
where the time goes in v1:
time: 47.7 us; the launch traced here: 47.5 us
  Pallas kernels  46.2 us (97%)
  local copies, waits for them, and re-layouts  1.35 us (3%)
    pallas_call x1, Pallas kernels, exchange(): pl.pallas_call(exchange_kernel, out_shape=jax.ShapeDtypeStruct((4, PLANE,...  38.4 us
    pallas_call x1, Pallas kernels, correlate(): pl.pallas_call(correlate_kernel, grid=(2,), out_shape=jax.ShapeDtypeStruc...  7.82 us

profile of v1, /device:TPU:1, one launch (start us, length us, event | category | flops | bytes accessed | tf_op | source)
XLA Modules:
  0.0 47.5 jit_solution(4728197851574287034)
XLA Ops:
  0.0 0.8 %copy.6 = s32[8,2]{1,0:T(8,128)S(1)} copy(s32[8,2]{0,1:T(2,128)} %param.6) | data formatting | bytes 128 | tf_op args[2]
  0.8 0.1 reshape.11
  0.8 0.5 %pad.4.tile_ref = s32[1,128]{1,0:T(1,128)} pad(s32[1,16]{1,0:T(1,128)S(1)} %reshape.11, s32[]{:T(128)} %constant.1.clone.1), padding=0_0x0_112 | pad | bytes 580 | tf_op jit(solution)/shard_map/jit(_pad)/pad | solution.py:240
  1.4 38.4 %exchange.1.blocks_ref = bf16[4,32,4,8,128]{4,3,2,1,0:T(8,128)(2,1)} custom-call(bf16[256,96]{1,0:T(8,128)(2,1)} %bitcast.2, s32[1,96]{1,0:T(1,128)} %bitcast.3, s32[1,128]{1,0:T(1,128)} %pad.4.tile_ref), custom_call_target="tpu_custom_call" | custom-call | tf_op jit(solution)/shard_map/exchange/pallas_call | solution.py:167
  39.7 7.8 %correlate.1 = f32[2,32,128,128]{3,2,1,0:T(8,128)} custom-call(bf16[4,32,4,8,128]{4,3,2,1,0:T(8,128)(2,1)} %exchange.1.blocks_ref, f32[17,2,1024]{2,1,0:T(2,128)} %constant.4.clone.table_ref), custom_call_target="tpu_custom_call" | custom-call | tf_op jit(solution)/shard_map/correlate/pallas_call | solution.py:220

commit v2 on v1

v2 whole, which is shorter than its diff:
```python
import math

import jax
import jax.numpy as jnp
import numpy as np
from jax import lax
from jax.experimental import pallas as pl
from jax.experimental.pallas import tpu as pltpu
from jax.sharding import PartitionSpec as P

F = 64
HOURS = 8
LAGS = 32
TILE = 128
EPSILON = 1e-06

PLANE = 32
SHARD = 96
HALF = 24
ROWS = 8
DEPTH = PLANE * ROWS
SLOTS = 4
FINE = 4
COARSE = LAGS // FINE
MESH_ID = pl.DeviceIdType.MESH


def fused_kernel(
    spec_hbm, bad_ref, tile_ref, left_table, right_table, out_ref,
    spec, white, mine, tiles_in, tiles, zb0, zb1, zb2, zb3, pack, got, cosines, sines, lhs, rhs,
    sem_in, sem_a_send, sem_a_recv, sem_t_send, sem_t_recv, sem_t_local, sem_z_send, sem_z_recv,
    sem_p_send, sem_p_recv,
):
    zbs = (zb0, zb1, zb2, zb3)
    chan, tm = lax.axis_index("chan"), lax.axis_index("tm")
    half = chan // PLANE
    me = chan % PLANE
    x, y, core = me // 8, (me // 2) % 4, me % 2
    z = half * 4 + tm

    load = pltpu.make_async_copy(spec_hbm, spec, sem_in)
    load.start()

    def plane_peer(j):
        dx, dy, dc = j // 8, (j // 2) % 4, j % 2
        k = ((x + dx) % 4) * 8 + ((y + dy) % 4) * 2 + (core + dc) % 2
        return k, (half * PLANE + k, tm)

    def plane(step):
        return (z + step) % 8

    def z_peer(step):
        return (plane(step) // 4) * PLANE + me, plane(step) % 4

    def base(step):
        return (plane(step) // 4) * HALF

    barrier = pltpu.get_barrier_semaphore()

    def greet(j, carry):
        _, dev = plane_peer(j)
        pl.semaphore_signal(barrier, inc=1, device_id=dev, device_id_type=MESH_ID)
        return carry

    lax.fori_loop(1, PLANE, greet, 0)
    for step in (2, 6, 1, 7):
        pl.semaphore_signal(barrier, inc=1, device_id=z_peer(step), device_id_type=MESH_ID)

    load.wait()
    values = spec[...].astype(jnp.float32).reshape(F // 2, ROWS, SHARD)
    squares = jnp.sum(values * values, axis=0)
    row = lax.broadcasted_iota(jnp.int32, (ROWS, SHARD), 0)
    first = (row % 4) < 2
    power0 = jnp.sum(jnp.where(first, squares, 0.0), axis=0, keepdims=True) / (2 * F)
    power1 = jnp.sum(jnp.where(first, 0.0, squares), axis=0, keepdims=True) / (2 * F)
    scale = lax.rsqrt(jnp.where(first, power0, power1) + EPSILON)
    keep = (1 - bad_ref[...]).astype(jnp.float32)
    whitened = values * scale[None] * keep[None]
    padded = jnp.concatenate([whitened, jnp.zeros((F // 2, ROWS, TILE - SHARD), jnp.float32)], axis=2)
    white[...] = padded.astype(jnp.bfloat16)

    pl.semaphore_wait(barrier, PLANE - 1 + 4)

    pltpu.make_async_copy(white.at[me], mine.at[me], sem_a_recv).start()

    def spread(j, carry):
        k, dev = plane_peer(j)
        pltpu.make_async_remote_copy(
            src_ref=white.at[k], dst_ref=mine.at[me], send_sem=sem_a_send, recv_sem=sem_a_recv,
            device_id=dev, device_id_type=MESH_ID,
        ).start()
        return carry

    lax.fori_loop(1, PLANE, spread, 0)

    pltpu.make_async_copy(tile_ref, tiles_in.at[me], sem_t_recv).start()

    def spread_tiles(j, carry):
        _, dev = plane_peer(j)
        pltpu.make_async_remote_copy(
            src_ref=tile_ref, dst_ref=tiles_in.at[me], send_sem=sem_t_send, recv_sem=sem_t_recv,
            device_id=dev, device_id_type=MESH_ID,
        ).start()
        return carry

    lax.fori_loop(1, PLANE, spread_tiles, 0)

    out_ref[...] = jnp.zeros_like(out_ref)
    for fine in range(1, FINE):
        column = 2 * (fine - 1)
        cosines[fine - 1] = jnp.broadcast_to(right_table[:, column : column + 1], (DEPTH, TILE))
        sines[fine - 1] = jnp.broadcast_to(right_table[:, column + 1 : column + 2], (DEPTH, TILE))

    pltpu.make_async_copy(mine, mine, sem_a_recv).wait()

    lane = lax.broadcasted_iota(jnp.int32, (ROWS, TILE), 1)
    own = half * HALF
    for g in range(PLANE // 4):
        s0, s1, s2, s3 = (mine[4 * g + i].astype(jnp.float32) for i in range(4))
        s1 = pltpu.roll(s1, 96, 1)
        s2 = pltpu.roll(s2, 64, 1)
        s3 = pltpu.roll(s3, 32, 1)
        zb3[own + 3 * g] = jnp.where(lane < 96, s0, s1).astype(jnp.bfloat16)
        zb3[own + 3 * g + 1] = jnp.where(lane < 64, s1, s2).astype(jnp.bfloat16)
        zb3[own + 3 * g + 2] = jnp.where(lane < 32, s2, s3).astype(jnp.bfloat16)

    def send_z(src, dst, chunk, at, count, step):
        pltpu.make_async_remote_copy(
            src_ref=src.at[pl.ds(at, count)], dst_ref=dst.at[pl.ds(at, count)],
            send_sem=sem_z_send, recv_sem=sem_z_recv.at[chunk],
            device_id=z_peer(step), device_id_type=MESH_ID,
        ).start()

    for step, chunk in ((2, 0), (6, 0), (7, 1), (1, 2)):
        send_z(zb3, zbs[chunk], chunk, own, HALF, step)

    pltpu.make_async_copy(tiles_in, tiles_in, sem_t_recv).wait()
    to_smem = pltpu.make_async_copy(tiles_in, tiles, sem_t_local)
    to_smem.start()
    to_smem.wait()

    for chunk in range(4):
        zb = zbs[chunk]
        if chunk < 3:
            pltpu.make_async_copy(zb, zb, sem_z_recv.at[chunk]).wait()
        else:
            other = zb.at[pl.ds((1 - half) * HALF, HALF)]
            pltpu.make_async_copy(other, other, sem_z_recv.at[chunk]).wait()
        if chunk == 0:
            send_z(zb0, zb1, 1, base(6), HALF, 1)
            send_z(zb0, zb2, 2, base(2), HALF, 7)
            send_z(zb0, zb3, 3, base(6), HALF // 2, 2)
            send_z(zb0, zb3, 3, base(2) + HALF // 2, HALF // 2, 6)

        def select(j, carry):
            k, _ = plane_peer(j)
            for s in range(SLOTS):
                pack[chunk, k, s] = zb[tiles[k, s % 2, 2 * tm + s // 2]]
            return carry

        lax.fori_loop(0, PLANE, select, 0)
        pltpu.make_async_copy(pack.at[chunk, me], got.at[chunk, me], sem_p_recv.at[chunk]).start()

        def deliver(j, carry):
            k, dev = plane_peer(j)
            pltpu.make_async_remote_copy(
                src_ref=pack.at[chunk, k], dst_ref=got.at[chunk, me],
                send_sem=sem_p_send, recv_sem=sem_p_recv.at[chunk],
                device_id=dev, device_id_type=MESH_ID,
            ).start()
            return carry

        lax.fori_loop(1, PLANE, deliver, 0)

    even_lane = lax.broadcasted_iota(jnp.int32, (TILE, TILE), 1) % 2 == 0
    even_row = lax.broadcasted_iota(jnp.int32, (PLANE, ROWS, TILE), 1) % 2 == 0

    def correlate(chunk, carry):
        part = got.at[chunk]
        pltpu.make_async_copy(part, part, sem_p_recv.at[chunk]).wait()

        def one_tile(i, carry):
            a = got[chunk, :, 2 * i].astype(jnp.float32).reshape(DEPTH, TILE)
            for h in range(DEPTH // TILE):
                block = a[h * TILE : (h + 1) * TILE].T
                turned = jnp.where(even_lane, -pltpu.roll(block, TILE - 1, 1), pltpu.roll(block, 1, 1))
                cols = pl.ds(h * TILE, TILE)
                for c in range(COARSE):
                    cos = left_table[2 * c : 2 * c + 1, h * TILE : (h + 1) * TILE]
                    sin = left_table[2 * c + 1 : 2 * c + 2, h * TILE : (h + 1) * TILE]
                    lhs[pl.ds(c * TILE, TILE), cols] = (block * cos + turned * sin).astype(jnp.bfloat16)
            b = got[chunk, :, 2 * i + 1].astype(jnp.float32)
            turned = jnp.where(even_row, pltpu.roll(b, ROWS - 1, 1), -pltpu.roll(b, 1, 1)).reshape(DEPTH, TILE)
            b = b.reshape(DEPTH, TILE)
            rhs[:, 0:TILE] = b.astype(jnp.bfloat16)
            for fine in range(1, FINE):
                rotated = b * cosines[fine - 1] + turned * sines[fine - 1]
                rhs[:, fine * TILE : (fine + 1) * TILE] = rotated.astype(jnp.bfloat16)
            for n in range(2):
                weights = rhs[:, 2 * n * TILE : (2 * n + 2) * TILE]
                for c in range(0, COARSE, 2):
                    res = jnp.dot(lhs[c * TILE : (c + 2) * TILE, :], weights, preferred_element_type=jnp.float32)
                    for dc in range(2):
                        for dn in range(2):
                            lag = FINE * (c + dc) + 2 * n + dn
                            out_ref[i, lag] += res[dc * TILE : (dc + 1) * TILE, dn * TILE : (dn + 1) * TILE]
            return carry

        return lax.fori_loop(0, 2, one_tile, carry)

    lax.fori_loop(0, 4, correlate, 0)

    sent = white.at[pl.ds(0, PLANE - 1)]
    pltpu.make_async_copy(sent, sent, sem_a_send).wait()
    sent = tiles_in.at[pl.ds(0, PLANE - 1)]
    pltpu.make_async_copy(sent, sent, sem_t_send).wait()
    for _ in range(7):
        sent = zb3.at[pl.ds(0, HALF)]
        pltpu.make_async_copy(sent, sent, sem_z_send).wait()
    sent = pack.at[:, pl.ds(0, PLANE - 1)]
    pltpu.make_async_copy(sent, sent, sem_p_send).wait()


def fused(spectra, bad, tile_pairs):
    vmem = pl.BlockSpec(memory_space=pltpu.VMEM)
    slab = pltpu.VMEM((2 * HALF, ROWS, TILE), jnp.bfloat16)
    dma = pltpu.SemaphoreType.DMA
    left_table, right_table = lag_tables()
    return pl.pallas_call(
        fused_kernel,
        out_shape=jax.ShapeDtypeStruct((2, LAGS, TILE, TILE), jnp.float32),
        in_specs=[pl.BlockSpec(memory_space=pl.ANY), vmem, vmem, vmem, vmem],
        out_specs=vmem,
        scratch_shapes=[
            pltpu.VMEM((F * 4, SHARD), jnp.bfloat16),
            pltpu.VMEM((PLANE, ROWS, TILE), jnp.bfloat16),
            pltpu.VMEM((PLANE, ROWS, TILE), jnp.bfloat16),
            pltpu.VMEM((PLANE, 2, 8), jnp.int32),
            pltpu.SMEM((PLANE, 2, 8), jnp.int32),
            slab, slab, slab, slab,
            pltpu.VMEM((4, PLANE, SLOTS, ROWS, TILE), jnp.bfloat16),
            pltpu.VMEM((4, PLANE, SLOTS, ROWS, TILE), jnp.bfloat16),
            pltpu.VMEM((FINE - 1, DEPTH, TILE), jnp.float32),
            pltpu.VMEM((FINE - 1, DEPTH, TILE), jnp.float32),
            pltpu.VMEM((COARSE * TILE, DEPTH), jnp.bfloat16),
            pltpu.VMEM((DEPTH, FINE * TILE), jnp.bfloat16),
            dma, dma, dma, dma, dma, dma, dma, dma((4,)), dma, dma((4,)),
        ],
        compiler_params=pltpu.CompilerParams(
            collective_id=0, has_side_effects=True, vmem_limit_bytes=16 << 20
        ),
        name="fused",
    )(spectra, bad, tile_pairs, jnp.asarray(left_table), jnp.asarray(right_table))


def lag_tables():
    row = np.arange(DEPTH)
    bin_number = 2 * (row // ROWS) + (row % ROWS) // 4 + 1.0
    angle = np.pi / F * bin_number
    coarse = FINE * np.arange(COARSE) - LAGS // 2
    norm = 1.0 / math.sqrt(F * HOURS)
    left = np.stack([np.cos(coarse[:, None] * angle), np.sin(coarse[:, None] * angle)], axis=1) * norm
    right = np.zeros((DEPTH, TILE))
    for fine in range(1, FINE):
        right[:, 2 * fine - 2] = np.cos(fine * angle)
        right[:, 2 * fine - 1] = np.sin(fine * angle)
    return left.reshape(2 * COARSE, DEPTH).astype(np.float32), right.astype(np.float32)


def per_device(spectra, bad_channels, tile_list):
    rows = spectra.reshape(F * 4, SHARD)
    return fused(rows, bad_channels.reshape(1, SHARD), tile_list.T)


def solution(mesh):
    placed = (P(None, "tm", None, "chan"), P("chan"), P("chan", None))
    return jax.shard_map(
        per_device,
        mesh=mesh,
        in_specs=placed,
        out_specs=P(("chan", "tm"), None, None, None),
        check_vma=False,
    )
```

time: 47.7 us -> 45 us (0.943)
  Pallas kernels: 46.2 us -> 39 us
  local copies, waits for them, and re-layouts: 1.35 us -> 5.81 us
    pallas_call x2 -> x1, Pallas kernels: 46.2 us -> 39 us  [fused(): pl.pallas_call(fused_kernel, out_shape=jax.ShapeDtypeStruct((2, LAGS, TIL...]
    unnamed x1 -> x11, local copies, waits for them, and re-layouts: 0.75 us -> 5.81 us
    pad x1 -> x0, local copies, waits for them, and re-layouts: 0.52 us -> none  [per_device(): tile_row = jnp.pad(tile_list.reshape(1, 16), ((0, 0), (0, TILE - 16)))]
where the time goes in v2:
time: 45 us; the launch traced here: 44.8 us
  Pallas kernels  39 us (87%)
  local copies, waits for them, and re-layouts  5.81 us (13%)
    pallas_call x1, Pallas kernels, fused(): pl.pallas_call(fused_kernel, out_shape=jax.ShapeDtypeStruct((2, LAGS, TIL...  39 us
    unnamed x11, local copies, waits for them, and re-layouts  5.81 us

profile of v2, /device:TPU:1, one launch (start us, length us, event | category | flops | bytes accessed | tf_op | source)
XLA Modules:
  0.0 44.8 jit_solution(17557090043232662365)
XLA Ops:
  0.0 0.0 copy-start
  0.0 0.9 %copy-done = f32[256,128]{1,0:T(8,128)S(1)} copy-done((f32[256,128]{1,0:T(8,128)S(1)}, f32[256,128]{1,0:T(8,128)}, u32[]{:S(2)}) %copy-start) | copy-done | bytes 131096
  0.9 0.0 copy-start.1
  0.9 0.8 %copy-done.1 = bf16[64,2,2,96]{3,2,1,0:T(2,128)(2,1)S(1)} copy-done((bf16[64,2,2,96]{3,2,1,0:T(2,128)(2,1)S(1)}, bf16[64,2,2,96]{3,2,1,0:T(2,128)(2,1)}, u32[]{:S(2)}) %copy-start.1) | copy-done | bytes 49176
  1.7 0.0 copy-start.2
  1.7 0.7 %copy-done.2 = f32[16,256]{1,0:T(8,128)S(1)} copy-done((f32[16,256]{1,0:T(8,128)S(1)}, f32[16,256]{1,0:T(8,128)}, u32[]{:S(2)}) %copy-start.2) | copy-done | bytes 16408
  2.5 0.0 copy-start.3
  2.5 0.7 %copy-done.3 = s32[8,2]{0,1:T(2,128)S(1)} copy-done((s32[8,2]{0,1:T(2,128)S(1)}, s32[8,2]{0,1:T(2,128)}, u32[]{:S(2)}) %copy-start.3) | copy-done | bytes 88
  3.1 0.0 copy-start.4
  3.1 0.7 %copy-done.4 = s32[96]{0:T(128)S(1)} copy-done((s32[96]{0:T(128)S(1)}, s32[96]{0:T(128)}, u32[]{:S(2)}) %copy-start.4) | copy-done | bytes 408
  3.8 39.0 %fused.1 = f32[2,32,128,128]{3,2,1,0:T(8,128)S(1)} custom-call(bf16[256,96]{1,0:T(8,128)(2,1)S(1)} %bitcast.3, s32[1,96]{1,0:T(1,128)S(1)} %bitcast.5, s32[2,8]{1,0:T(2,128)S(1)} %bitcast.4, f32[16,256]{1,0:T(8,128)S(1)} %copy-done.2, f32[256,128]{1,0:T(8,128)S(1)} %copy-done), custom_call_target="tpu_custom_call" | custom-call | tf_op jit(solution)/shard_map/fused/pallas_call | solution.py:229
  42.8 2.0 %copy.7 = f32[2,32,128,128]{3,2,1,0:T(8,128)} copy(f32[2,32,128,128]{3,2,1,0:T(8,128)S(1)} %fused.1) | data formatting | bytes 8388608
Async XLA Ops:
  0.0 0.9 %copy-start = (f32[256,128]{1,0:T(8,128)S(1)}, f32[256,128]{1,0:T(8,128)}, u32[]{:S(2)}) copy-start(f32[256,128]{1,0:T(8,128)} %constant.5.clone.right_table) | copy-start | bytes 393220
  0.9 0.8 %copy-start.1 = (bf16[64,2,2,96]{3,2,1,0:T(2,128)(2,1)S(1)}, bf16[64,2,2,96]{3,2,1,0:T(2,128)(2,1)}, u32[]{:S(2)}) copy-start(bf16[64,2,2,96]{3,2,1,0:T(2,128)(2,1)} %param.5) | copy-start | bytes 147460
  1.7 0.7 %copy-start.2 = (f32[16,256]{1,0:T(8,128)S(1)}, f32[16,256]{1,0:T(8,128)}, u32[]{:S(2)}) copy-start(f32[16,256]{1,0:T(8,128)} %constant.4.clone.left_table) | copy-start | bytes 49156
  2.5 0.7 %copy-start.3 = (s32[8,2]{0,1:T(2,128)S(1)}, s32[8,2]{0,1:T(2,128)}, u32[]{:S(2)}) copy-start(s32[8,2]{0,1:T(2,128)} %param.7) | copy-start | bytes 196
  3.1 0.7 %copy-start.4 = (s32[96]{0:T(128)S(1)}, s32[96]{0:T(128)}, u32[]{:S(2)}) copy-start(s32[96]{0:T(128)} %param.6) | copy-start | bytes 1156

commit v3 on v2

--- a/solution.py
+++ b/solution.py
@@ -22,51 +22,68 @@
 SLOTS = 4
 FINE = 4
 COARSE = LAGS // FINE
+FAR = 20
 MESH_ID = pl.DeviceIdType.MESH
 
 
 def fused_kernel(
-    spec_hbm, bad_ref, tile_ref, left_table, right_table, out_ref,
-    spec, white, mine, tiles_in, tiles, zb0, zb1, zb2, zb3, pack, got, cosines, sines, lhs, rhs,
+    spec_hbm, bad_hbm, tile_hbm, left_hbm, right_hbm, out_ref,
+    spec, bad_ref, tile_ref, left_table, right_table, white, mine, tiles_in, tiles, zb0, zb1, zb2, zb3, pack, got, cosines, sines, lhs, rhs,
     sem_in, sem_a_send, sem_a_recv, sem_t_send, sem_t_recv, sem_t_local, sem_z_send, sem_z_recv,
     sem_p_send, sem_p_recv,
 ):
     zbs = (zb0, zb1, zb2, zb3)
     chan, tm = lax.axis_index("chan"), lax.axis_index("tm")
-    half = chan // PLANE
-    me = chan % PLANE
-    x, y, core = me // 8, (me // 2) % 4, me % 2
+    half = lax.shift_right_logical(chan, 5)
+    me = lax.bitwise_and(chan, PLANE - 1)
     z = half * 4 + tm
 
-    load = pltpu.make_async_copy(spec_hbm, spec, sem_in)
-    load.start()
+    loads = [
+        pltpu.make_async_copy(src, dst, sem_in.at[i])
+        for i, (src, dst) in enumerate(
+            ((spec_hbm, spec), (bad_hbm, bad_ref), (tile_hbm, tile_ref), (left_hbm, left_table), (right_hbm, right_table))
+        )
+    ]
+    for load in loads:
+        load.start()
 
     def plane_peer(j):
-        dx, dy, dc = j // 8, (j // 2) % 4, j % 2
-        k = ((x + dx) % 4) * 8 + ((y + dy) % 4) * 2 + (core + dc) % 2
-        return k, (half * PLANE + k, tm)
+        k = lax.bitwise_xor(me, j)
+        return k, (lax.bitwise_xor(chan, j), tm)
+
+    def each_peer(act):
+        def four(i, carry):
+            for u in range(4):
+                act(lax.bitwise_xor(4 * i + u, FAR))
+            return carry
+
+        lax.fori_loop(0, FAR // 4, four, 0)
+        for u in range(FAR + 1, FAR + 4):
+            act(u ^ FAR)
+        lax.fori_loop(FAR // 4 + 1, PLANE // 4, four, 0)
 
     def plane(step):
-        return (z + step) % 8
+        return lax.bitwise_and(z + step, 7)
 
     def z_peer(step):
-        return (plane(step) // 4) * PLANE + me, plane(step) % 4
+        zz = plane(step)
+        return lax.shift_right_logical(zz, 2) * PLANE + me, lax.bitwise_and(zz, 3)
 
     def base(step):
-        return (plane(step) // 4) * HALF
+        return lax.shift_right_logical(plane(step), 2) * HALF
 
     barrier = pltpu.get_barrier_semaphore()
 
-    def greet(j, carry):
+    def greet(j):
         _, dev = plane_peer(j)
         pl.semaphore_signal(barrier, inc=1, device_id=dev, device_id_type=MESH_ID)
-        return carry
-
-    lax.fori_loop(1, PLANE, greet, 0)
+
+    each_peer(greet)
     for step in (2, 6, 1, 7):
         pl.semaphore_signal(barrier, inc=1, device_id=z_peer(step), device_id_type=MESH_ID)
 
-    load.wait()
+    for load in loads[:2]:
+        load.wait()
     values = spec[...].astype(jnp.float32).reshape(F // 2, ROWS, SHARD)
     squares = jnp.sum(values * values, axis=0)
     row = lax.broadcasted_iota(jnp.int32, (ROWS, SHARD), 0)
@@ -83,27 +100,27 @@
 
     pltpu.make_async_copy(white.at[me], mine.at[me], sem_a_recv).start()
 
-    def spread(j, carry):
+    def spread(j):
         k, dev = plane_peer(j)
         pltpu.make_async_remote_copy(
             src_ref=white.at[k], dst_ref=mine.at[me], send_sem=sem_a_send, recv_sem=sem_a_recv,
             device_id=dev, device_id_type=MESH_ID,
         ).start()
-        return carry
-
-    lax.fori_loop(1, PLANE, spread, 0)
-
+
+    each_peer(spread)
+
+    for load in loads[2:]:
+        load.wait()
     pltpu.make_async_copy(tile_ref, tiles_in.at[me], sem_t_recv).start()
 
-    def spread_tiles(j, carry):
+    def spread_tiles(j):
         _, dev = plane_peer(j)
         pltpu.make_async_remote_copy(
             src_ref=tile_ref, dst_ref=tiles_in.at[me], send_sem=sem_t_send, recv_sem=sem_t_recv,
             device_id=dev, device_id_type=MESH_ID,
         ).start()
-        return carry
-
-    lax.fori_loop(1, PLANE, spread_tiles, 0)
+
+    each_peer(spread_tiles)
 
     out_ref[...] = jnp.zeros_like(out_ref)
     for fine in range(1, FINE):
@@ -152,25 +169,25 @@
             send_z(zb0, zb3, 3, base(6), HALF // 2, 2)
             send_z(zb0, zb3, 3, base(2) + HALF // 2, HALF // 2, 6)
 
-        def select(j, carry):
-            k, _ = plane_peer(j)
-            for s in range(SLOTS):
-                pack[chunk, k, s] = zb[tiles[k, s % 2, 2 * tm + s // 2]]
+        def select(i, carry):
+            places = [(4 * i + u, s) for u in range(4) for s in range(SLOTS)]
+            blocks = [zb[tiles[k, s % 2, 2 * tm + s // 2]] for k, s in places]
+            for (k, s), block in zip(places, blocks):
+                pack[chunk, k, s] = block
             return carry
 
-        lax.fori_loop(0, PLANE, select, 0)
+        lax.fori_loop(0, PLANE // 4, select, 0)
         pltpu.make_async_copy(pack.at[chunk, me], got.at[chunk, me], sem_p_recv.at[chunk]).start()
 
-        def deliver(j, carry):
+        def deliver(j):
             k, dev = plane_peer(j)
             pltpu.make_async_remote_copy(
                 src_ref=pack.at[chunk, k], dst_ref=got.at[chunk, me],
                 send_sem=sem_p_send, recv_sem=sem_p_recv.at[chunk],
                 device_id=dev, device_id_type=MESH_ID,
             ).start()
-            return carry
-
-        lax.fori_loop(1, PLANE, deliver, 0)
+
+        each_peer(deliver)
 
     even_lane = lax.broadcasted_iota(jnp.int32, (TILE, TILE), 1) % 2 == 0
     even_row = lax.broadcasted_iota(jnp.int32, (PLANE, ROWS, TILE), 1) % 2 == 0
@@ -229,10 +246,14 @@
     return pl.pallas_call(
         fused_kernel,
         out_shape=jax.ShapeDtypeStruct((2, LAGS, TILE, TILE), jnp.float32),
-        in_specs=[pl.BlockSpec(memory_space=pl.ANY), vmem, vmem, vmem, vmem],
+        in_specs=[pl.BlockSpec(memory_space=pltpu.HBM)] * 5,
         out_specs=vmem,
         scratch_shapes=[
             pltpu.VMEM((F * 4, SHARD), jnp.bfloat16),
+            pltpu.VMEM((1, SHARD), jnp.int32),
+            pltpu.VMEM((2, 8), jnp.int32),
+            pltpu.VMEM((2 * COARSE, DEPTH), jnp.float32),
+            pltpu.VMEM((DEPTH, TILE), jnp.float32),
             pltpu.VMEM((PLANE, ROWS, TILE), jnp.bfloat16),
             pltpu.VMEM((PLANE, ROWS, TILE), jnp.bfloat16),
             pltpu.VMEM((PLANE, 2, 8), jnp.int32),
@@ -244,13 +265,13 @@
             pltpu.VMEM((FINE - 1, DEPTH, TILE), jnp.float32),
             pltpu.VMEM((COARSE * TILE, DEPTH), jnp.bfloat16),
             pltpu.VMEM((DEPTH, FINE * TILE), jnp.bfloat16),
-            dma, dma, dma, dma, dma, dma, dma, dma((4,)), dma, dma((4,)),
+            dma((5,)), dma, dma, dma, dma, dma, dma, dma((4,)), dma, dma((4,)),
         ],
         compiler_params=pltpu.CompilerParams(
             collective_id=0, has_side_effects=True, vmem_limit_bytes=16 << 20
         ),
         name="fused",
-    )(spectra, bad, tile_pairs, jnp.asarray(left_table), jnp.asarray(right_table))
+    )(*(pltpu.with_memory_space_constraint(v, pltpu.HBM) for v in (spectra, bad, tile_pairs, jnp.asarray(left_table), jnp.asarray(right_table))))
 
 
 def lag_tables():

time: 45 us -> 38.7 us (0.86)
  local copies, waits for them, and re-layouts: 5.81 us -> 2.02 us
  Pallas kernels: 39 us -> 36.6 us
    unnamed x11 -> x1, local copies, waits for them, and re-layouts: 5.81 us -> 2.02 us
    pallas_call x1, Pallas kernels: 39 us -> 36.6 us  [fused(): pl.pallas_call(fused_kernel, out_shape=jax.ShapeDtypeStruct((2, LAGS, TIL...]
where the time goes in v3:
time: 38.7 us; the launch traced here: 38.6 us
  Pallas kernels  36.6 us (95%)
  local copies, waits for them, and re-layouts  2.02 us (5%)
    pallas_call x1, Pallas kernels, fused(): pl.pallas_call(fused_kernel, out_shape=jax.ShapeDtypeStruct((2, LAGS, TIL...  36.6 us
    unnamed x1, local copies, waits for them, and re-layouts  2.02 us

profile of v3, /device:TPU:1, one launch (start us, length us, event | category | flops | bytes accessed | tf_op | source)
XLA Modules:
  0.0 38.6 jit_solution(15483916544147178923)
XLA Ops:
  0.0 36.6 %fused.1 = f32[2,32,128,128]{3,2,1,0:T(8,128)S(1)} custom-call(bf16[256,96]{1,0:T(8,128)(2,1)} %bitcast.3, s32[1,96]{1,0:T(1,128)} %bitcast.5, s32[2,8]{1,0:T(2,128)} %bitcast.4, f32[16,256]{1,0:T(8,128)} %constant.4.clone.left_hbm, f32[256,128]{1,0:T(8,128)} %constant.5.clone.right_hbm), custom_call_target="tpu_custom_call" | custom-call | tf_op jit(solution)/shard_map/fused/pallas_call | solution.py:246
  36.6 2.0 %copy.7 = f32[2,32,128,128]{3,2,1,0:T(8,128)} copy(f32[2,32,128,128]{3,2,1,0:T(8,128)S(1)} %fused.1) | data formatting | bytes 8388608

commit v4 on v3

--- a/solution.py
+++ b/solution.py
@@ -23,12 +23,15 @@
 FINE = 4
 COARSE = LAGS // FINE
 FAR = 20
+NEAR = (0, 2, 6, 8, 24)
+CROSS = tuple((near + dc, dc) for near in NEAR for dc in range(2))
+INSIDE = tuple(j for j in range(PLANE) if (j & ~1) ^ FAR not in NEAR)
 MESH_ID = pl.DeviceIdType.MESH
 
 
 def fused_kernel(
     spec_hbm, bad_hbm, tile_hbm, left_hbm, right_hbm, out_ref,
-    spec, bad_ref, tile_ref, left_table, right_table, white, mine, tiles_in, tiles, zb0, zb1, zb2, zb3, pack, got, cosines, sines, lhs, rhs,
+    spec, bad_ref, tile_ref, left_table, right_table, white, mine, tiles_in, tiles, zb0, zb1, zb2, zb3, pack, got, cosines, sines, lhs, rhs, other,
     sem_in, sem_a_send, sem_a_recv, sem_t_send, sem_t_recv, sem_t_local, sem_z_send, sem_z_recv,
     sem_p_send, sem_p_recv,
 ):
@@ -37,6 +40,7 @@
     half = lax.shift_right_logical(chan, 5)
     me = lax.bitwise_and(chan, PLANE - 1)
     z = half * 4 + tm
+    odd = lax.bitwise_and(z, 1)
 
     loads = [
         pltpu.make_async_copy(src, dst, sem_in.at[i])
@@ -65,9 +69,9 @@
     def plane(step):
         return lax.bitwise_and(z + step, 7)
 
-    def z_peer(step):
+    def z_peer(step, j=0):
         zz = plane(step)
-        return lax.shift_right_logical(zz, 2) * PLANE + me, lax.bitwise_and(zz, 3)
+        return lax.shift_right_logical(zz, 2) * PLANE + lax.bitwise_xor(me, j), lax.bitwise_and(zz, 3)
 
     def base(step):
         return lax.shift_right_logical(plane(step), 2) * HALF
@@ -79,8 +83,8 @@
         pl.semaphore_signal(barrier, inc=1, device_id=dev, device_id_type=MESH_ID)
 
     each_peer(greet)
-    for step in (2, 6, 1, 7):
-        pl.semaphore_signal(barrier, inc=1, device_id=z_peer(step), device_id_type=MESH_ID)
+    for step, j in [(3, 0), (5, 0), (2, 0), (6, 0)] + [(step, j) for j, _ in CROSS for step in (1, 7)]:
+        pl.semaphore_signal(barrier, inc=1, device_id=z_peer(step, j), device_id_type=MESH_ID)
 
     for load in loads[:2]:
         load.wait()
@@ -94,9 +98,12 @@
     keep = (1 - bad_ref[...]).astype(jnp.float32)
     whitened = values * scale[None] * keep[None]
     padded = jnp.concatenate([whitened, jnp.zeros((F // 2, ROWS, TILE - SHARD), jnp.float32)], axis=2)
-    white[...] = padded.astype(jnp.bfloat16)
-
-    pl.semaphore_wait(barrier, PLANE - 1 + 4)
+    padded = padded.astype(jnp.bfloat16)
+    white[:, 0] = padded
+    for g in range(PLANE // 4):
+        white[pl.ds((4 * g) ^ FAR, 4), 1] = padded[4 * g : 4 * g + 4]
+
+    pl.semaphore_wait(barrier, PLANE - 1 + 4 + 2 * len(CROSS))
 
     pltpu.make_async_copy(white.at[me], mine.at[me], sem_a_recv).start()
 
@@ -111,16 +118,18 @@
 
     for load in loads[2:]:
         load.wait()
-    pltpu.make_async_copy(tile_ref, tiles_in.at[me], sem_t_recv).start()
-
-    def spread_tiles(j):
-        _, dev = plane_peer(j)
+    pltpu.make_async_copy(tile_ref, tiles_in.at[0], sem_t_recv).start()
+
+    def send_tiles(slot, dev):
         pltpu.make_async_remote_copy(
-            src_ref=tile_ref, dst_ref=tiles_in.at[me], send_sem=sem_t_send, recv_sem=sem_t_recv,
+            src_ref=tile_ref, dst_ref=tiles_in.at[slot], send_sem=sem_t_send, recv_sem=sem_t_recv,
             device_id=dev, device_id_type=MESH_ID,
         ).start()
 
-    each_peer(spread_tiles)
+    for n, j in enumerate(INSIDE[1:], 1):
+        send_tiles(n, plane_peer(j)[1])
+    for n, (j, dc) in enumerate(CROSS, len(INSIDE)):
+        send_tiles(n, z_peer((1, 7)[dc], j))
 
     out_ref[...] = jnp.zeros_like(out_ref)
     for fine in range(1, FINE):
@@ -132,29 +141,48 @@
 
     lane = lax.broadcasted_iota(jnp.int32, (ROWS, TILE), 1)
     own = half * HALF
-    for g in range(PLANE // 4):
-        s0, s1, s2, s3 = (mine[4 * g + i].astype(jnp.float32) for i in range(4))
-        s1 = pltpu.roll(s1, 96, 1)
-        s2 = pltpu.roll(s2, 64, 1)
-        s3 = pltpu.roll(s3, 32, 1)
-        zb3[own + 3 * g] = jnp.where(lane < 96, s0, s1).astype(jnp.bfloat16)
-        zb3[own + 3 * g + 1] = jnp.where(lane < 64, s1, s2).astype(jnp.bfloat16)
-        zb3[own + 3 * g + 2] = jnp.where(lane < 32, s2, s3).astype(jnp.bfloat16)
+
+    def to_blocks(kind, dst, start):
+        for g in range(PLANE // 4):
+            s0, s1, s2, s3 = (mine[4 * g + i, kind].astype(jnp.float32) for i in range(4))
+            s1 = pltpu.roll(s1, 96, 1)
+            s2 = pltpu.roll(s2, 64, 1)
+            s3 = pltpu.roll(s3, 32, 1)
+            dst[start + 3 * g] = jnp.where(lane < 96, s0, s1).astype(jnp.bfloat16)
+            dst[start + 3 * g + 1] = jnp.where(lane < 64, s1, s2).astype(jnp.bfloat16)
+            dst[start + 3 * g + 2] = jnp.where(lane < 32, s2, s3).astype(jnp.bfloat16)
 
     def send_z(src, dst, chunk, at, count, step):
         pltpu.make_async_remote_copy(
-            src_ref=src.at[pl.ds(at, count)], dst_ref=dst.at[pl.ds(at, count)],
+            src_ref=src, dst_ref=dst.at[pl.ds(at, count)],
             send_sem=sem_z_send, recv_sem=sem_z_recv.at[chunk],
             device_id=z_peer(step), device_id_type=MESH_ID,
         ).start()
 
-    for step, chunk in ((2, 0), (6, 0), (7, 1), (1, 2)):
-        send_z(zb3, zbs[chunk], chunk, own, HALF, step)
+    to_blocks(odd, zb3, own)
+    for step in (2, 6):
+        send_z(zb3.at[pl.ds(own, HALF)], zb0, 0, own, HALF, step)
+    to_blocks(1 - odd, other, 0)
+    for step, chunk in ((7, 1), (3, 1), (1, 2), (5, 2)):
+        send_z(other, zbs[chunk], chunk, own, HALF, step)
 
     pltpu.make_async_copy(tiles_in, tiles_in, sem_t_recv).wait()
     to_smem = pltpu.make_async_copy(tiles_in, tiles, sem_t_local)
     to_smem.start()
     to_smem.wait()
+
+    slot = lax.bitwise_xor(me, odd * FAR)
+    wanted = [(plane_peer(j)[1], tm) for j in INSIDE]
+    for j, dc in CROSS:
+        dev = z_peer((7, 1)[dc], j)
+        wanted.append((dev, dev[1]))
+
+    def deliver(chunk, n):
+        pltpu.make_async_remote_copy(
+            src_ref=pack.at[chunk, n], dst_ref=got.at[chunk, slot],
+            send_sem=sem_p_send, recv_sem=sem_p_recv.at[chunk],
+            device_id=wanted[n][0], device_id_type=MESH_ID,
+        ).start()
 
     for chunk in range(4):
         zb = zbs[chunk]
@@ -164,30 +192,20 @@
             other = zb.at[pl.ds((1 - half) * HALF, HALF)]
             pltpu.make_async_copy(other, other, sem_z_recv.at[chunk]).wait()
         if chunk == 0:
-            send_z(zb0, zb1, 1, base(6), HALF, 1)
-            send_z(zb0, zb2, 2, base(2), HALF, 7)
-            send_z(zb0, zb3, 3, base(6), HALF // 2, 2)
-            send_z(zb0, zb3, 3, base(2) + HALF // 2, HALF // 2, 6)
-
-        def select(i, carry):
-            places = [(4 * i + u, s) for u in range(4) for s in range(SLOTS)]
-            blocks = [zb[tiles[k, s % 2, 2 * tm + s // 2]] for k, s in places]
-            for (k, s), block in zip(places, blocks):
-                pack[chunk, k, s] = block
-            return carry
-
-        lax.fori_loop(0, PLANE // 4, select, 0)
-        pltpu.make_async_copy(pack.at[chunk, me], got.at[chunk, me], sem_p_recv.at[chunk]).start()
-
-        def deliver(j):
-            k, dev = plane_peer(j)
-            pltpu.make_async_remote_copy(
-                src_ref=pack.at[chunk, k], dst_ref=got.at[chunk, me],
-                send_sem=sem_p_send, recv_sem=sem_p_recv.at[chunk],
-                device_id=dev, device_id_type=MESH_ID,
-            ).start()
-
-        each_peer(deliver)
+            for step, at in ((2, base(6)), (6, base(2) + HALF // 2)):
+                send_z(zb0.at[pl.ds(at, HALF // 2)], zb3, 3, at, HALF // 2, step)
+
+        if chunk == 1:
+            for n in range(len(INSIDE), PLANE):
+                deliver(0, n)
+        for n in range(0, PLANE, 4):
+            places = [(n + u, s) for u in range(4) for s in range(SLOTS)]
+            blocks = [zb[tiles[i, s % 2, 2 * wanted[i][1] + s // 2]] for i, s in places]
+            for (i, s), block in zip(places, blocks):
+                pack[chunk, i, s] = block
+        pltpu.make_async_copy(pack.at[chunk, 0], got.at[chunk, slot], sem_p_recv.at[chunk]).start()
+        for n in reversed(range(1, len(INSIDE) if chunk == 0 else PLANE)):
+            deliver(chunk, n)
 
     even_lane = lax.broadcasted_iota(jnp.int32, (TILE, TILE), 1) % 2 == 0
     even_row = lax.broadcasted_iota(jnp.int32, (PLANE, ROWS, TILE), 1) % 2 == 0
@@ -254,8 +272,8 @@
             pltpu.VMEM((2, 8), jnp.int32),
             pltpu.VMEM((2 * COARSE, DEPTH), jnp.float32),
             pltpu.VMEM((DEPTH, TILE), jnp.float32),
-            pltpu.VMEM((PLANE, ROWS, TILE), jnp.bfloat16),
-            pltpu.VMEM((PLANE, ROWS, TILE), jnp.bfloat16),
+            pltpu.VMEM((PLANE, 2, ROWS, TILE), jnp.bfloat16),
+            pltpu.VMEM((PLANE, 2, ROWS, TILE), jnp.bfloat16),
             pltpu.VMEM((PLANE, 2, 8), jnp.int32),
             pltpu.SMEM((PLANE, 2, 8), jnp.int32),
             slab, slab, slab, slab,
@@ -265,6 +283,7 @@
             pltpu.VMEM((FINE - 1, DEPTH, TILE), jnp.float32),
             pltpu.VMEM((COARSE * TILE, DEPTH), jnp.bfloat16),
             pltpu.VMEM((DEPTH, FINE * TILE), jnp.bfloat16),
+            pltpu.VMEM((HALF, ROWS, TILE), jnp.bfloat16),
             dma((5,)), dma, dma, dma, dma, dma, dma, dma((4,)), dma, dma((4,)),
         ],
         compiler_params=pltpu.CompilerParams(

time: 38.7 us -> 36.3 us (0.938)
  Pallas kernels: 36.6 us -> 34.2 us
    pallas_call x1, Pallas kernels: 36.6 us -> 34.2 us  [fused(): pl.pallas_call(fused_kernel, out_shape=jax.ShapeDtypeStruct((2, LAGS, TIL...]
where the time goes in v4:
time: 36.3 us; the launch traced here: 36.2 us
  Pallas kernels  34.2 us (94%)
  local copies, waits for them, and re-layouts  2.02 us (6%)
    pallas_call x1, Pallas kernels, fused(): pl.pallas_call(fused_kernel, out_shape=jax.ShapeDtypeStruct((2, LAGS, TIL...  34.2 us
    unnamed x1, local copies, waits for them, and re-layouts  2.02 us

profile of v4, /device:TPU:1, one launch (start us, length us, event | category | flops | bytes accessed | tf_op | source)
XLA Modules:
  0.0 36.2 jit_solution(18390445579446804662)
XLA Ops:
  0.0 34.2 %fused.1 = f32[2,32,128,128]{3,2,1,0:T(8,128)S(1)} custom-call(bf16[256,96]{1,0:T(8,128)(2,1)} %bitcast.3, s32[1,96]{1,0:T(1,128)} %bitcast.5, s32[2,8]{1,0:T(2,128)} %bitcast.4, f32[16,256]{1,0:T(8,128)} %constant.4.clone.left_hbm, f32[256,128]{1,0:T(8,128)} %constant.5.clone.right_hbm), custom_call_target="tpu_custom_call" | custom-call | tf_op jit(solution)/shard_map/fused/pallas_call | solution.py:264
  34.2 2.0 %copy.7 = f32[2,32,128,128]{3,2,1,0:T(8,128)} copy(f32[2,32,128,128]{3,2,1,0:T(8,128)S(1)} %fused.1) | data formatting | bytes 8388608

commit v5 on v4

--- a/solution.py
+++ b/solution.py
@@ -29,10 +29,57 @@
 MESH_ID = pl.DeviceIdType.MESH
 
 
+def load_blocks(got, i, left_table, cosines, sines, lhs, rhs):
+    even_lane = lax.broadcasted_iota(jnp.int32, (TILE, TILE), 1) % 2 == 0
+    even_row = lax.broadcasted_iota(jnp.int32, (PLANE, ROWS, TILE), 1) % 2 == 0
+    a = got[:, 2 * i].astype(jnp.float32).reshape(DEPTH, TILE)
+    for h in range(DEPTH // TILE):
+        block = a[h * TILE : (h + 1) * TILE].T
+        turned = jnp.where(even_lane, -pltpu.roll(block, TILE - 1, 1), pltpu.roll(block, 1, 1))
+        cols = pl.ds(h * TILE, TILE)
+        for c in range(COARSE):
+            cos = left_table[2 * c : 2 * c + 1, h * TILE : (h + 1) * TILE]
+            sin = left_table[2 * c + 1 : 2 * c + 2, h * TILE : (h + 1) * TILE]
+            lhs[pl.ds(c * TILE, TILE), cols] = (block * cos + turned * sin).astype(jnp.bfloat16)
+    b = got[:, 2 * i + 1].astype(jnp.float32)
+    turned = jnp.where(even_row, pltpu.roll(b, ROWS - 1, 1), -pltpu.roll(b, 1, 1)).reshape(DEPTH, TILE)
+    b = b.reshape(DEPTH, TILE)
+    rhs[:, 0:TILE] = b.astype(jnp.bfloat16)
+    for fine in range(1, FINE):
+        rotated = b * cosines[fine - 1] + turned * sines[fine - 1]
+        rhs[:, fine * TILE : (fine + 1) * TILE] = rotated.astype(jnp.bfloat16)
+
+
+def lag_products(lhs, rhs, c, add):
+    for n in range(2):
+        weights = rhs[:, 2 * n * TILE : (2 * n + 2) * TILE]
+        res = jnp.dot(lhs[c * TILE : (c + 2) * TILE, :], weights, preferred_element_type=jnp.float32)
+        for dc in range(2):
+            for dn in range(2):
+                lag = FINE * (c + dc) + 2 * n + dn
+                add(lag, res[dc * TILE : (dc + 1) * TILE, dn * TILE : (dn + 1) * TILE])
+
+
+def finish_kernel(last, partial, left_table, cosines, sines, out_hbm, stage, lhs, rhs, sems):
+    copies = []
+    for i in range(2):
+        load_blocks(last, i, left_table, cosines, sines, lhs.at[i], rhs.at[i])
+        for c in range(0, COARSE, 2):
+            def put(lag, value):
+                stage[i, lag] = partial[i, lag] + value
+
+            lag_products(lhs.at[i], rhs.at[i], c, put)
+            lags = pl.ds(FINE * c, 2 * FINE)
+            copies.append(pltpu.make_async_copy(stage.at[i, lags], out_hbm.at[i, lags], sems.at[len(copies)]))
+            copies[-1].start()
+    for copy in copies:
+        copy.wait()
+
+
 def fused_kernel(
-    spec_hbm, bad_hbm, tile_hbm, left_hbm, right_hbm, out_ref,
-    spec, bad_ref, tile_ref, left_table, right_table, white, mine, tiles_in, tiles, zb0, zb1, zb2, zb3, pack, got, cosines, sines, lhs, rhs, other,
-    sem_in, sem_a_send, sem_a_recv, sem_t_send, sem_t_recv, sem_t_local, sem_z_send, sem_z_recv,
+    spec_hbm, bad_hbm, tile_hbm, left_hbm, right_hbm, out_ref, last, left_table, cosines, sines,
+    spec, bad_ref, tile_ref, right_table, white, mine, mine_other, tiles_in, tiles, zb0, zb1, zb2, zb3, pack, got, lhs, rhs, other,
+    sem_in, sem_a_send, sem_a_recv, sem_b_recv, sem_t_send, sem_t_recv, sem_t_local, sem_z_send, sem_z_recv,
     sem_p_send, sem_p_recv,
 ):
     zbs = (zb0, zb1, zb2, zb3)
@@ -99,22 +146,22 @@
     whitened = values * scale[None] * keep[None]
     padded = jnp.concatenate([whitened, jnp.zeros((F // 2, ROWS, TILE - SHARD), jnp.float32)], axis=2)
     padded = padded.astype(jnp.bfloat16)
-    white[:, 0] = padded
-    for g in range(PLANE // 4):
-        white[pl.ds((4 * g) ^ FAR, 4), 1] = padded[4 * g : 4 * g + 4]
+    white[...] = padded
 
     pl.semaphore_wait(barrier, PLANE - 1 + 4 + 2 * len(CROSS))
 
-    pltpu.make_async_copy(white.at[me], mine.at[me], sem_a_recv).start()
-
-    def spread(j):
-        k, dev = plane_peer(j)
-        pltpu.make_async_remote_copy(
-            src_ref=white.at[k], dst_ref=mine.at[me], send_sem=sem_a_send, recv_sem=sem_a_recv,
-            device_id=dev, device_id_type=MESH_ID,
-        ).start()
-
-    each_peer(spread)
+    for kind, dst, sem in ((odd, mine, sem_a_recv), (1 - odd, mine_other, sem_b_recv)):
+        shift = kind * FAR
+        pltpu.make_async_copy(white.at[lax.bitwise_xor(me, shift)], dst.at[me], sem).start()
+
+        def spread(j):
+            k, dev = plane_peer(j)
+            pltpu.make_async_remote_copy(
+                src_ref=white.at[lax.bitwise_xor(k, shift)], dst_ref=dst.at[me], send_sem=sem_a_send, recv_sem=sem,
+                device_id=dev, device_id_type=MESH_ID,
+            ).start()
+
+        each_peer(spread)
 
     for load in loads[2:]:
         load.wait()
@@ -137,14 +184,12 @@
         cosines[fine - 1] = jnp.broadcast_to(right_table[:, column : column + 1], (DEPTH, TILE))
         sines[fine - 1] = jnp.broadcast_to(right_table[:, column + 1 : column + 2], (DEPTH, TILE))
 
-    pltpu.make_async_copy(mine, mine, sem_a_recv).wait()
-
     lane = lax.broadcasted_iota(jnp.int32, (ROWS, TILE), 1)
     own = half * HALF
 
-    def to_blocks(kind, dst, start):
+    def to_blocks(src, dst, start):
         for g in range(PLANE // 4):
-            s0, s1, s2, s3 = (mine[4 * g + i, kind].astype(jnp.float32) for i in range(4))
+            s0, s1, s2, s3 = (src[4 * g + i].astype(jnp.float32) for i in range(4))
             s1 = pltpu.roll(s1, 96, 1)
             s2 = pltpu.roll(s2, 64, 1)
             s3 = pltpu.roll(s3, 32, 1)
@@ -159,10 +204,12 @@
             device_id=z_peer(step), device_id_type=MESH_ID,
         ).start()
 
-    to_blocks(odd, zb3, own)
+    pltpu.make_async_copy(mine, mine, sem_a_recv).wait()
+    to_blocks(mine, zb3, own)
     for step in (2, 6):
         send_z(zb3.at[pl.ds(own, HALF)], zb0, 0, own, HALF, step)
-    to_blocks(1 - odd, other, 0)
+    pltpu.make_async_copy(mine_other, mine_other, sem_b_recv).wait()
+    to_blocks(mine_other, other, 0)
     for step, chunk in ((7, 1), (3, 1), (1, 2), (5, 2)):
         send_z(other, zbs[chunk], chunk, own, HALF, step)
 
@@ -177,20 +224,20 @@
         dev = z_peer((7, 1)[dc], j)
         wanted.append((dev, dev[1]))
 
+    def landing(chunk):
+        return got.at[chunk, slot] if chunk < 3 else last.at[slot]
+
     def deliver(chunk, n):
         pltpu.make_async_remote_copy(
-            src_ref=pack.at[chunk, n], dst_ref=got.at[chunk, slot],
+            src_ref=pack.at[chunk, n], dst_ref=landing(chunk),
             send_sem=sem_p_send, recv_sem=sem_p_recv.at[chunk],
             device_id=wanted[n][0], device_id_type=MESH_ID,
         ).start()
 
     for chunk in range(4):
         zb = zbs[chunk]
-        if chunk < 3:
-            pltpu.make_async_copy(zb, zb, sem_z_recv.at[chunk]).wait()
-        else:
-            other = zb.at[pl.ds((1 - half) * HALF, HALF)]
-            pltpu.make_async_copy(other, other, sem_z_recv.at[chunk]).wait()
+        late = zb if chunk < 3 else zb.at[pl.ds(base(4), HALF)]
+        pltpu.make_async_copy(late, late, sem_z_recv.at[chunk]).wait()
         if chunk == 0:
             for step, at in ((2, base(6)), (6, base(2) + HALF // 2)):
                 send_z(zb0.at[pl.ds(at, HALF // 2)], zb3, 3, at, HALF // 2, step)
@@ -203,50 +250,31 @@
             blocks = [zb[tiles[i, s % 2, 2 * wanted[i][1] + s // 2]] for i, s in places]
             for (i, s), block in zip(places, blocks):
                 pack[chunk, i, s] = block
-        pltpu.make_async_copy(pack.at[chunk, 0], got.at[chunk, slot], sem_p_recv.at[chunk]).start()
+        pltpu.make_async_copy(pack.at[chunk, 0], landing(chunk), sem_p_recv.at[chunk]).start()
         for n in reversed(range(1, len(INSIDE) if chunk == 0 else PLANE)):
             deliver(chunk, n)
-
-    even_lane = lax.broadcasted_iota(jnp.int32, (TILE, TILE), 1) % 2 == 0
-    even_row = lax.broadcasted_iota(jnp.int32, (PLANE, ROWS, TILE), 1) % 2 == 0
 
     def correlate(chunk, carry):
         part = got.at[chunk]
         pltpu.make_async_copy(part, part, sem_p_recv.at[chunk]).wait()
 
         def one_tile(i, carry):
-            a = got[chunk, :, 2 * i].astype(jnp.float32).reshape(DEPTH, TILE)
-            for h in range(DEPTH // TILE):
-                block = a[h * TILE : (h + 1) * TILE].T
-                turned = jnp.where(even_lane, -pltpu.roll(block, TILE - 1, 1), pltpu.roll(block, 1, 1))
-                cols = pl.ds(h * TILE, TILE)
-                for c in range(COARSE):
-                    cos = left_table[2 * c : 2 * c + 1, h * TILE : (h + 1) * TILE]
-                    sin = left_table[2 * c + 1 : 2 * c + 2, h * TILE : (h + 1) * TILE]
-                    lhs[pl.ds(c * TILE, TILE), cols] = (block * cos + turned * sin).astype(jnp.bfloat16)
-            b = got[chunk, :, 2 * i + 1].astype(jnp.float32)
-            turned = jnp.where(even_row, pltpu.roll(b, ROWS - 1, 1), -pltpu.roll(b, 1, 1)).reshape(DEPTH, TILE)
-            b = b.reshape(DEPTH, TILE)
-            rhs[:, 0:TILE] = b.astype(jnp.bfloat16)
-            for fine in range(1, FINE):
-                rotated = b * cosines[fine - 1] + turned * sines[fine - 1]
-                rhs[:, fine * TILE : (fine + 1) * TILE] = rotated.astype(jnp.bfloat16)
-            for n in range(2):
-                weights = rhs[:, 2 * n * TILE : (2 * n + 2) * TILE]
-                for c in range(0, COARSE, 2):
-                    res = jnp.dot(lhs[c * TILE : (c + 2) * TILE, :], weights, preferred_element_type=jnp.float32)
-                    for dc in range(2):
-                        for dn in range(2):
-                            lag = FINE * (c + dc) + 2 * n + dn
-                            out_ref[i, lag] += res[dc * TILE : (dc + 1) * TILE, dn * TILE : (dn + 1) * TILE]
+            def add(lag, value):
+                out_ref[i, lag] += value
+
+            load_blocks(part, i, left_table, cosines, sines, lhs, rhs)
+            for c in range(0, COARSE, 2):
+                lag_products(lhs, rhs, c, add)
             return carry
 
         return lax.fori_loop(0, 2, one_tile, carry)
 
-    lax.fori_loop(0, 4, correlate, 0)
-
+    lax.fori_loop(0, 3, correlate, 0)
+
+    pltpu.make_async_copy(last, last, sem_p_recv.at[3]).wait()
     sent = white.at[pl.ds(0, PLANE - 1)]
-    pltpu.make_async_copy(sent, sent, sem_a_send).wait()
+    for _ in range(2):
+        pltpu.make_async_copy(sent, sent, sem_a_send).wait()
     sent = tiles_in.at[pl.ds(0, PLANE - 1)]
     pltpu.make_async_copy(sent, sent, sem_t_send).wait()
     for _ in range(7):
@@ -261,36 +289,59 @@
     slab = pltpu.VMEM((2 * HALF, ROWS, TILE), jnp.bfloat16)
     dma = pltpu.SemaphoreType.DMA
     left_table, right_table = lag_tables()
-    return pl.pallas_call(
+    block = (PLANE, SLOTS, ROWS, TILE)
+    table = (FINE - 1, DEPTH, TILE)
+    partial, *rest = pl.pallas_call(
         fused_kernel,
-        out_shape=jax.ShapeDtypeStruct((2, LAGS, TILE, TILE), jnp.float32),
+        out_shape=[
+            jax.ShapeDtypeStruct((2, LAGS, TILE, TILE), jnp.float32),
+            jax.ShapeDtypeStruct(block, jnp.bfloat16),
+            jax.ShapeDtypeStruct((2 * COARSE, DEPTH), jnp.float32),
+            jax.ShapeDtypeStruct(table, jnp.float32),
+            jax.ShapeDtypeStruct(table, jnp.float32),
+        ],
         in_specs=[pl.BlockSpec(memory_space=pltpu.HBM)] * 5,
-        out_specs=vmem,
+        out_specs=[vmem] * 5,
         scratch_shapes=[
             pltpu.VMEM((F * 4, SHARD), jnp.bfloat16),
             pltpu.VMEM((1, SHARD), jnp.int32),
             pltpu.VMEM((2, 8), jnp.int32),
-            pltpu.VMEM((2 * COARSE, DEPTH), jnp.float32),
             pltpu.VMEM((DEPTH, TILE), jnp.float32),
-            pltpu.VMEM((PLANE, 2, ROWS, TILE), jnp.bfloat16),
-            pltpu.VMEM((PLANE, 2, ROWS, TILE), jnp.bfloat16),
+            pltpu.VMEM((PLANE, ROWS, TILE), jnp.bfloat16),
+            pltpu.VMEM((PLANE, ROWS, TILE), jnp.bfloat16),
+            pltpu.VMEM((PLANE, ROWS, TILE), jnp.bfloat16),
             pltpu.VMEM((PLANE, 2, 8), jnp.int32),
             pltpu.SMEM((PLANE, 2, 8), jnp.int32),
             slab, slab, slab, slab,
-            pltpu.VMEM((4, PLANE, SLOTS, ROWS, TILE), jnp.bfloat16),
-            pltpu.VMEM((4, PLANE, SLOTS, ROWS, TILE), jnp.bfloat16),
-            pltpu.VMEM((FINE - 1, DEPTH, TILE), jnp.float32),
-            pltpu.VMEM((FINE - 1, DEPTH, TILE), jnp.float32),
+            pltpu.VMEM((4, *block), jnp.bfloat16),
+            pltpu.VMEM((3, *block), jnp.bfloat16),
             pltpu.VMEM((COARSE * TILE, DEPTH), jnp.bfloat16),
             pltpu.VMEM((DEPTH, FINE * TILE), jnp.bfloat16),
             pltpu.VMEM((HALF, ROWS, TILE), jnp.bfloat16),
-            dma((5,)), dma, dma, dma, dma, dma, dma, dma((4,)), dma, dma((4,)),
+            dma((5,)), dma, dma, dma, dma, dma, dma, dma, dma((4,)), dma, dma((4,)),
         ],
         compiler_params=pltpu.CompilerParams(
             collective_id=0, has_side_effects=True, vmem_limit_bytes=16 << 20
         ),
         name="fused",
-    )(*(pltpu.with_memory_space_constraint(v, pltpu.HBM) for v in (spectra, bad, tile_pairs, jnp.asarray(left_table), jnp.asarray(right_table))))
+    )(*(
+        pltpu.with_memory_space_constraint(v, pltpu.HBM)
+        for v in (spectra, bad, tile_pairs, jnp.asarray(left_table), jnp.asarray(right_table))
+    ))
+    return pl.pallas_call(
+        finish_kernel,
+        out_shape=jax.ShapeDtypeStruct((2, LAGS, TILE, TILE), jnp.float32),
+        in_specs=[vmem] * 5,
+        out_specs=pl.BlockSpec(memory_space=pltpu.HBM),
+        scratch_shapes=[
+            pltpu.VMEM((2, LAGS, TILE, TILE), jnp.float32),
+            pltpu.VMEM((2, COARSE * TILE, DEPTH), jnp.bfloat16),
+            pltpu.VMEM((2, DEPTH, FINE * TILE), jnp.bfloat16),
+            dma((COARSE,)),
+        ],
+        compiler_params=pltpu.CompilerParams(vmem_limit_bytes=12 << 20),
+        name="finish",
+    )(rest[0], partial, *rest[1:])
 
 
 def lag_tables():

time: 36.3 us -> 35.5 us (0.978)
  local copies, waits for them, and re-layouts: 2.02 us -> 0 us
  Pallas kernels: 34.2 us -> 35.4 us
    unnamed x1 -> x0, local copies, waits for them, and re-layouts: 2.02 us -> none
    pallas_call x1 -> x2, Pallas kernels: 34.2 us -> 35.4 us  [the longest x1 32.8 us: fused(): pl.pallas_call(fused_kernel, out_shape=[jax.ShapeDtypeStruct((2, LAGS, TI...]
where the time goes in v5:
time: 35.5 us; the launch traced here: 35.4 us
  Pallas kernels  35.4 us (100%)
    pallas_call x1, Pallas kernels, fused(): pl.pallas_call(fused_kernel, out_shape=[jax.ShapeDtypeStruct((2, LAGS, TI...  32.8 us
    pallas_call x1, Pallas kernels, fused(): pl.pallas_call(finish_kernel, out_shape=jax.ShapeDtypeStruct((2, LAGS, TI...  2.66 us

profile of v5, /device:TPU:1, one launch (start us, length us, event | category | flops | bytes accessed | tf_op | source)
XLA Modules:
  0.0 35.4 jit_solution(9338088593101323890)
XLA Ops:
  0.0 32.8 %fused.1 = (f32[2,32,128,128]{3,2,1,0:T(8,128)S(1)}, bf16[32,4,8,128]{3,2,1,0:T(8,128)(2,1)S(1)}, f32[16,256]{1,0:T(8,128)S(1)}, f32[3,256,128]{2,1,0:T(8,128)S(1)}, f32[3,256,128]{2,1,0:T(8,128)S(1)}) custom-call(bf16[256,96]{1,0:T(8,128)(2,1)} %bitcast.3, s32[1,96]{1,0:T(1,128)} %bitcast.5, s32[2,8]{1,0:T(2,128)} %bitcast.4, ...), custom_call_target="tpu_custom_call" | custom-call | tf_op jit(solution)/shard_map/fused/pallas_call | solution.py:294
  32.8 2.7 %finish.1 = f32[2,32,128,128]{3,2,1,0:T(8,128)} custom-call(bf16[32,4,8,128]{3,2,1,0:T(8,128)(2,1)S(1)} %get-tuple-element.10.last, f32[2,32,128,128]{3,2,1,0:T(8,128)S(1)} %get-tuple-element.11.partial, f32[16,256]{1,0:T(8,128)S(1)} %get-tuple-element.12.left_table, f32[3,256,128]{2,1,0:T(8,128)S(1)} %get-tuple-element.13.cosines, ...), custom_call_target="tpu_custom_call" | custom-call | tf_op jit(solution)/shard_map/finish/pallas_call | solution.py:331

commit v6 on v5

--- a/solution.py
+++ b/solution.py
@@ -29,22 +29,17 @@
 MESH_ID = pl.DeviceIdType.MESH
 
 
-def load_blocks(got, i, left_table, cosines, sines, lhs, rhs):
-    even_lane = lax.broadcasted_iota(jnp.int32, (TILE, TILE), 1) % 2 == 0
-    even_row = lax.broadcasted_iota(jnp.int32, (PLANE, ROWS, TILE), 1) % 2 == 0
-    a = got[:, 2 * i].astype(jnp.float32).reshape(DEPTH, TILE)
-    for h in range(DEPTH // TILE):
-        block = a[h * TILE : (h + 1) * TILE].T
-        turned = jnp.where(even_lane, -pltpu.roll(block, TILE - 1, 1), pltpu.roll(block, 1, 1))
-        cols = pl.ds(h * TILE, TILE)
-        for c in range(COARSE):
-            cos = left_table[2 * c : 2 * c + 1, h * TILE : (h + 1) * TILE]
-            sin = left_table[2 * c + 1 : 2 * c + 2, h * TILE : (h + 1) * TILE]
-            lhs[pl.ds(c * TILE, TILE), cols] = (block * cos + turned * sin).astype(jnp.bfloat16)
-    b = got[:, 2 * i + 1].astype(jnp.float32)
-    turned = jnp.where(even_row, pltpu.roll(b, ROWS - 1, 1), -pltpu.roll(b, 1, 1)).reshape(DEPTH, TILE)
-    b = b.reshape(DEPTH, TILE)
-    rhs[:, 0:TILE] = b.astype(jnp.bfloat16)
+def load_blocks(got, i, left_table, cosines, sines, swap, eye, lhs, rhs):
+    a = got[:, 2 * i].astype(jnp.float32).reshape(DEPTH, TILE).astype(jnp.bfloat16)
+    a = lax.dot_general(eye[...], a, (((1,), (1,)), ((), ())), preferred_element_type=jnp.float32)
+    turned = jnp.dot(a.astype(jnp.bfloat16), swap[...], preferred_element_type=jnp.float32)
+    for c in range(COARSE):
+        rotated = a * left_table[2 * c : 2 * c + 1] + turned * left_table[2 * c + 1 : 2 * c + 2]
+        lhs[pl.ds(c * TILE, TILE)] = rotated.astype(jnp.bfloat16)
+    b = got[:, 2 * i + 1].astype(jnp.float32).reshape(DEPTH, TILE)
+    exact = b.astype(jnp.bfloat16)
+    turned = jnp.dot(swap[...], exact, preferred_element_type=jnp.float32)
+    rhs[:, 0:TILE] = exact
     for fine in range(1, FINE):
         rotated = b * cosines[fine - 1] + turned * sines[fine - 1]
         rhs[:, fine * TILE : (fine + 1) * TILE] = rotated.astype(jnp.bfloat16)
@@ -60,10 +55,10 @@
                 add(lag, res[dc * TILE : (dc + 1) * TILE, dn * TILE : (dn + 1) * TILE])
 
 
-def finish_kernel(last, partial, left_table, cosines, sines, out_hbm, stage, lhs, rhs, sems):
+def finish_kernel(last, partial, left_table, cosines, sines, swap, eye, out_hbm, stage, lhs, rhs, sems):
     copies = []
     for i in range(2):
-        load_blocks(last, i, left_table, cosines, sines, lhs.at[i], rhs.at[i])
+        load_blocks(last, i, left_table, cosines, sines, swap, eye, lhs.at[i], rhs.at[i])
         for c in range(0, COARSE, 2):
             def put(lag, value):
                 stage[i, lag] = partial[i, lag] + value
@@ -77,7 +72,7 @@
 
 
 def fused_kernel(
-    spec_hbm, bad_hbm, tile_hbm, left_hbm, right_hbm, out_ref, last, left_table, cosines, sines,
+    spec_hbm, bad_hbm, tile_hbm, left_hbm, right_hbm, out_ref, last, left_table, cosines, sines, swap, eye,
     spec, bad_ref, tile_ref, right_table, white, mine, mine_other, tiles_in, tiles, zb0, zb1, zb2, zb3, pack, got, lhs, rhs, other,
     sem_in, sem_a_send, sem_a_recv, sem_b_recv, sem_t_send, sem_t_recv, sem_t_local, sem_z_send, sem_z_recv,
     sem_p_send, sem_p_recv,
@@ -179,6 +174,12 @@
         send_tiles(n, z_peer((1, 7)[dc], j))
 
     out_ref[...] = jnp.zeros_like(out_ref)
+    row = lax.broadcasted_iota(jnp.int32, (DEPTH, DEPTH), 0)
+    ahead = lax.broadcasted_iota(jnp.int32, (DEPTH, DEPTH), 1) - row
+    even = lax.bitwise_and(row, 1) == 0
+    to_re = jnp.where(even, jnp.where(ahead == 1, 1.0, 0.0), jnp.where(ahead == -1, -1.0, 0.0))
+    swap[...] = to_re.astype(jnp.bfloat16)
+    eye[...] = jnp.where(ahead[:TILE, :TILE] == 0, 1.0, 0.0).astype(jnp.bfloat16)
     for fine in range(1, FINE):
         column = 2 * (fine - 1)
         cosines[fine - 1] = jnp.broadcast_to(right_table[:, column : column + 1], (DEPTH, TILE))
@@ -262,7 +263,7 @@
             def add(lag, value):
                 out_ref[i, lag] += value
 
-            load_blocks(part, i, left_table, cosines, sines, lhs, rhs)
+            load_blocks(part, i, left_table, cosines, sines, swap, eye, lhs, rhs)
             for c in range(0, COARSE, 2):
                 lag_products(lhs, rhs, c, add)
             return carry
@@ -299,9 +300,11 @@
             jax.ShapeDtypeStruct((2 * COARSE, DEPTH), jnp.float32),
             jax.ShapeDtypeStruct(table, jnp.float32),
             jax.ShapeDtypeStruct(table, jnp.float32),
+            jax.ShapeDtypeStruct((DEPTH, DEPTH), jnp.bfloat16),
+            jax.ShapeDtypeStruct((TILE, TILE), jnp.bfloat16),
         ],
         in_specs=[pl.BlockSpec(memory_space=pltpu.HBM)] * 5,
-        out_specs=[vmem] * 5,
+        out_specs=[vmem] * 7,
         scratch_shapes=[
             pltpu.VMEM((F * 4, SHARD), jnp.bfloat16),
             pltpu.VMEM((1, SHARD), jnp.int32),
@@ -331,7 +334,7 @@
     return pl.pallas_call(
         finish_kernel,
         out_shape=jax.ShapeDtypeStruct((2, LAGS, TILE, TILE), jnp.float32),
-        in_specs=[vmem] * 5,
+        in_specs=[vmem] * 7,
         out_specs=pl.BlockSpec(memory_space=pltpu.HBM),
         scratch_shapes=[
             pltpu.VMEM((2, LAGS, TILE, TILE), jnp.float32),

time: 35.5 us -> 35.5 us (level)
  no operation moved by 1% of the time
where the time goes in v6:
time: 35.5 us; the launch traced here: 35.4 us
  Pallas kernels  35.4 us (100%)
    pallas_call x1, Pallas kernels, fused(): pl.pallas_call(fused_kernel, out_shape=[jax.ShapeDtypeStruct((2, LAGS, TI...  32.8 us
    pallas_call x1, Pallas kernels, fused(): pl.pallas_call(finish_kernel, out_shape=jax.ShapeDtypeStruct((2, LAGS, TI...  2.58 us

profile of v6, /device:TPU:1, one launch (start us, length us, event | category | flops | bytes accessed | tf_op | source)
XLA Modules:
  0.0 35.4 jit_solution(6221868187500244120)
XLA Ops:
  0.0 32.8 %fused.1 = (f32[2,32,128,128]{3,2,1,0:T(8,128)S(1)}, bf16[32,4,8,128]{3,2,1,0:T(8,128)(2,1)S(1)}, f32[16,256]{1,0:T(8,128)S(1)}, f32[3,256,128]{2,1,0:T(8,128)S(...) custom-call(bf16[256,96]{1,0:T(8,128)(2,1)} %bitcast.3, ...), custom_call_target="tpu_custom_call" | custom-call | tf_op jit(solution)/shard_map/fused/pallas_call | solution.py:295
  32.8 2.6 %finish.1 = f32[2,32,128,128]{3,2,1,0:T(8,128)} custom-call(bf16[32,4,8,128]{3,2,1,0:T(8,128)(2,1)S(1)} %get-tuple-element.12.last, f32[2,32,128,128]{3,2,1,0:T(8,128)S(1)} %get-tuple-element.13.partial, f32[16,256]{1,0:T(8,128)S(1)} %get-tuple-element.14.left_table, f32[3,256,128]{2,1,0:T(8,128)S(1)} %get-tuple-element.15.cosines, ...), custom_call_target="tpu_custom_call" | custom-call | tf_op jit(solution)/shard_map/finish/pallas_call | solution.py:334

commit v7 on v6

--- a/solution.py
+++ b/solution.py
@@ -26,23 +26,38 @@
 NEAR = (0, 2, 6, 8, 24)
 CROSS = tuple((near + dc, dc) for near in NEAR for dc in range(2))
 INSIDE = tuple(j for j in range(PLANE) if (j & ~1) ^ FAR not in NEAR)
+PIECE = ROWS // 2
+ROUNDS = (((0, 0), (0, 1)), ((1, 0), (2, 0)), ((1, 1), (2, 1)), ((3, 0), (3, 1)))
 MESH_ID = pl.DeviceIdType.MESH
 
 
-def load_blocks(got, i, left_table, cosines, sines, swap, eye, lhs, rhs):
-    a = got[:, 2 * i].astype(jnp.float32).reshape(DEPTH, TILE).astype(jnp.bfloat16)
-    a = lax.dot_general(eye[...], a, (((1,), (1,)), ((), ())), preferred_element_type=jnp.float32)
+def load_blocks(got, i, bins, left_table, cosines, sines, swap, eye, lhs, rhs):
+    starts = [pl.multiple_of(TILE * f, TILE) for f in bins]
+
+    def block(side):
+        halves = [got[:, h, 2 * i + side].astype(jnp.float32).reshape(TILE, TILE) for h in range(2)]
+        return jnp.concatenate(halves, axis=0)
+
+    a = lax.dot_general(
+        eye[...], block(0).astype(jnp.bfloat16), (((1,), (1,)), ((), ())), preferred_element_type=jnp.float32
+    )
     turned = jnp.dot(a.astype(jnp.bfloat16), swap[...], preferred_element_type=jnp.float32)
-    for c in range(COARSE):
-        rotated = a * left_table[2 * c : 2 * c + 1] + turned * left_table[2 * c + 1 : 2 * c + 2]
-        lhs[pl.ds(c * TILE, TILE)] = rotated.astype(jnp.bfloat16)
-    b = got[:, 2 * i + 1].astype(jnp.float32).reshape(DEPTH, TILE)
+    for h, start in enumerate(starts):
+        cols = slice(h * TILE, (h + 1) * TILE)
+        for c in range(COARSE):
+            cos = left_table[2 * c : 2 * c + 1, pl.ds(start, TILE)]
+            sin = left_table[2 * c + 1 : 2 * c + 2, pl.ds(start, TILE)]
+            lhs[pl.ds(c * TILE, TILE), cols] = (a[:, cols] * cos + turned[:, cols] * sin).astype(jnp.bfloat16)
+    b = block(1)
     exact = b.astype(jnp.bfloat16)
     turned = jnp.dot(swap[...], exact, preferred_element_type=jnp.float32)
     rhs[:, 0:TILE] = exact
-    for fine in range(1, FINE):
-        rotated = b * cosines[fine - 1] + turned * sines[fine - 1]
-        rhs[:, fine * TILE : (fine + 1) * TILE] = rotated.astype(jnp.bfloat16)
+    for h, start in enumerate(starts):
+        rows = slice(h * TILE, (h + 1) * TILE)
+        for fine in range(1, FINE):
+            cos = cosines[fine - 1, pl.ds(start, TILE)]
+            sin = sines[fine - 1, pl.ds(start, TILE)]
+            rhs[rows, fine * TILE : (fine + 1) * TILE] = (b[rows] * cos + turned[rows] * sin).astype(jnp.bfloat16)
 
 
 def lag_products(lhs, rhs, c, add):
@@ -58,7 +73,7 @@
 def finish_kernel(last, partial, left_table, cosines, sines, swap, eye, out_hbm, stage, lhs, rhs, sems):
     copies = []
     for i in range(2):
-        load_blocks(last, i, left_table, cosines, sines, swap, eye, lhs.at[i], rhs.at[i])
+        load_blocks(last, i, (0, 1), left_table, cosines, sines, swap, eye, lhs.at[i], rhs.at[i])
         for c in range(0, COARSE, 2):
             def put(lag, value):
                 stage[i, lag] = partial[i, lag] + value
@@ -73,11 +88,11 @@
 
 def fused_kernel(
     spec_hbm, bad_hbm, tile_hbm, left_hbm, right_hbm, out_ref, last, left_table, cosines, sines, swap, eye,
-    spec, bad_ref, tile_ref, right_table, white, mine, mine_other, tiles_in, tiles, zb0, zb1, zb2, zb3, pack, got, lhs, rhs, other,
+    spec, bad_ref, tile_ref, right_table, white, mine, mine_other, tiles_in, tiles, zb00, zb01, zb10, zb11, zb20, zb21, zb30, zb31, pack, got, lhs, rhs, other0, other1,
     sem_in, sem_a_send, sem_a_recv, sem_b_recv, sem_t_send, sem_t_recv, sem_t_local, sem_z_send, sem_z_recv,
     sem_p_send, sem_p_recv,
 ):
-    zbs = (zb0, zb1, zb2, zb3)
+    zbs = ((zb00, zb01), (zb10, zb11), (zb20, zb21), (zb30, zb31))
     chan, tm = lax.axis_index("chan"), lax.axis_index("tm")
     half = lax.shift_right_logical(chan, 5)
     me = lax.bitwise_and(chan, PLANE - 1)
@@ -194,25 +209,29 @@
             s1 = pltpu.roll(s1, 96, 1)
             s2 = pltpu.roll(s2, 64, 1)
             s3 = pltpu.roll(s3, 32, 1)
-            dst[start + 3 * g] = jnp.where(lane < 96, s0, s1).astype(jnp.bfloat16)
-            dst[start + 3 * g + 1] = jnp.where(lane < 64, s1, s2).astype(jnp.bfloat16)
-            dst[start + 3 * g + 2] = jnp.where(lane < 32, s2, s3).astype(jnp.bfloat16)
-
-    def send_z(src, dst, chunk, at, count, step):
+            for n, merged in enumerate(
+                (jnp.where(lane < 96, s0, s1), jnp.where(lane < 64, s1, s2), jnp.where(lane < 32, s2, s3))
+            ):
+                for f in range(2):
+                    dst[f][start + 3 * g + n] = merged[f * PIECE : (f + 1) * PIECE].astype(jnp.bfloat16)
+
+    def send_z(src, chunk, f, at, count, step):
         pltpu.make_async_remote_copy(
-            src_ref=src, dst_ref=dst.at[pl.ds(at, count)],
-            send_sem=sem_z_send, recv_sem=sem_z_recv.at[chunk],
+            src_ref=src, dst_ref=zbs[chunk][f].at[pl.ds(at, count)],
+            send_sem=sem_z_send, recv_sem=sem_z_recv.at[chunk, f],
             device_id=z_peer(step), device_id_type=MESH_ID,
         ).start()
 
     pltpu.make_async_copy(mine, mine, sem_a_recv).wait()
-    to_blocks(mine, zb3, own)
-    for step in (2, 6):
-        send_z(zb3.at[pl.ds(own, HALF)], zb0, 0, own, HALF, step)
+    to_blocks(mine, zbs[3], own)
+    for f in range(2):
+        for step in (2, 6):
+            send_z(zbs[3][f].at[pl.ds(own, HALF)], 0, f, own, HALF, step)
     pltpu.make_async_copy(mine_other, mine_other, sem_b_recv).wait()
-    to_blocks(mine_other, other, 0)
-    for step, chunk in ((7, 1), (3, 1), (1, 2), (5, 2)):
-        send_z(other, zbs[chunk], chunk, own, HALF, step)
+    to_blocks(mine_other, (other0, other1), 0)
+    for f, other in enumerate((other0, other1)):
+        for step, chunk in ((7, 1), (3, 1), (1, 2), (5, 2)):
+            send_z(other, chunk, f, own, HALF, step)
 
     pltpu.make_async_copy(tiles_in, tiles_in, sem_t_recv).wait()
     to_smem = pltpu.make_async_copy(tiles_in, tiles, sem_t_local)
@@ -225,35 +244,39 @@
         dev = z_peer((7, 1)[dc], j)
         wanted.append((dev, dev[1]))
 
-    def landing(chunk):
-        return got.at[chunk, slot] if chunk < 3 else last.at[slot]
-
-    def deliver(chunk, n):
+    def landing(n):
+        return got.at[n, slot] if n < 3 else last.at[slot]
+
+    def deliver(src, dst, n, to):
         pltpu.make_async_remote_copy(
-            src_ref=pack.at[chunk, n], dst_ref=landing(chunk),
-            send_sem=sem_p_send, recv_sem=sem_p_recv.at[chunk],
-            device_id=wanted[n][0], device_id_type=MESH_ID,
+            src_ref=src, dst_ref=dst, send_sem=sem_p_send, recv_sem=sem_p_recv.at[n],
+            device_id=wanted[to][0], device_id_type=MESH_ID,
         ).start()
 
-    for chunk in range(4):
-        zb = zbs[chunk]
-        late = zb if chunk < 3 else zb.at[pl.ds(base(4), HALF)]
-        pltpu.make_async_copy(late, late, sem_z_recv.at[chunk]).wait()
-        if chunk == 0:
-            for step, at in ((2, base(6)), (6, base(2) + HALF // 2)):
-                send_z(zb0.at[pl.ds(at, HALF // 2)], zb3, 3, at, HALF // 2, step)
-
-        if chunk == 1:
-            for n in range(len(INSIDE), PLANE):
-                deliver(0, n)
-        for n in range(0, PLANE, 4):
-            places = [(n + u, s) for u in range(4) for s in range(SLOTS)]
-            blocks = [zb[tiles[i, s % 2, 2 * wanted[i][1] + s // 2]] for i, s in places]
-            for (i, s), block in zip(places, blocks):
-                pack[chunk, i, s] = block
-        pltpu.make_async_copy(pack.at[chunk, 0], landing(chunk), sem_p_recv.at[chunk]).start()
-        for n in reversed(range(1, len(INSIDE) if chunk == 0 else PLANE)):
-            deliver(chunk, n)
+    for n, pieces in enumerate(ROUNDS):
+        whole = pieces[0][0] == pieces[1][0]
+        for h, (chunk, f) in enumerate(pieces):
+            zb = zbs[chunk][f]
+            late = zb if chunk < 3 else zb.at[pl.ds(base(4), HALF)]
+            pltpu.make_async_copy(late, late, sem_z_recv.at[chunk, f]).wait()
+            if chunk == 0:
+                for step, at in ((2, base(6)), (6, base(2) + HALF // 2)):
+                    send_z(zb.at[pl.ds(at, HALF // 2)], 3, f, at, HALF // 2, step)
+            for to in range(0, PLANE, 4):
+                places = [(to + u, s) for u in range(4) for s in range(SLOTS)]
+                blocks = [zb[tiles[i, s % 2, 2 * wanted[i][1] + s // 2]] for i, s in places]
+                for (i, s), block in zip(places, blocks):
+                    pack[n, i, h, s] = block
+            if n == 1 and h == 0:
+                for to in range(len(INSIDE), PLANE):
+                    deliver(pack.at[0, to], landing(0), 0, to)
+            if not whole:
+                for to in reversed(range(1, PLANE)):
+                    deliver(pack.at[n, to, h], landing(n).at[h], n, to)
+        pltpu.make_async_copy(pack.at[n, 0], landing(n), sem_p_recv.at[n]).start()
+        if whole:
+            for to in reversed(range(1, len(INSIDE) if n == 0 else PLANE)):
+                deliver(pack.at[n, to], landing(n), n, to)
 
     def correlate(chunk, carry):
         part = got.at[chunk]
@@ -263,7 +286,8 @@
             def add(lag, value):
                 out_ref[i, lag] += value
 
-            load_blocks(part, i, left_table, cosines, sines, swap, eye, lhs, rhs)
+            bins = (lax.shift_right_logical(chunk, 1), 1 - lax.bitwise_and(chunk, 1))
+            load_blocks(part, i, bins, left_table, cosines, sines, swap, eye, lhs, rhs)
             for c in range(0, COARSE, 2):
                 lag_products(lhs, rhs, c, add)
             return carry
@@ -279,18 +303,19 @@
     sent = tiles_in.at[pl.ds(0, PLANE - 1)]
     pltpu.make_async_copy(sent, sent, sem_t_send).wait()
     for _ in range(7):
-        sent = zb3.at[pl.ds(0, HALF)]
-        pltpu.make_async_copy(sent, sent, sem_z_send).wait()
+        for f in range(2):
+            sent = zbs[3][f].at[pl.ds(0, HALF)]
+            pltpu.make_async_copy(sent, sent, sem_z_send).wait()
     sent = pack.at[:, pl.ds(0, PLANE - 1)]
     pltpu.make_async_copy(sent, sent, sem_p_send).wait()
 
 
 def fused(spectra, bad, tile_pairs):
     vmem = pl.BlockSpec(memory_space=pltpu.VMEM)
-    slab = pltpu.VMEM((2 * HALF, ROWS, TILE), jnp.bfloat16)
+    slab = pltpu.VMEM((2 * HALF, PIECE, TILE), jnp.bfloat16)
     dma = pltpu.SemaphoreType.DMA
     left_table, right_table = lag_tables()
-    block = (PLANE, SLOTS, ROWS, TILE)
+    block = (PLANE, 2, SLOTS, PIECE, TILE)
     table = (FINE - 1, DEPTH, TILE)
     partial, *rest = pl.pallas_call(
         fused_kernel,
@@ -315,13 +340,14 @@
             pltpu.VMEM((PLANE, ROWS, TILE), jnp.bfloat16),
             pltpu.VMEM((PLANE, 2, 8), jnp.int32),
             pltpu.SMEM((PLANE, 2, 8), jnp.int32),
-            slab, slab, slab, slab,
+            slab, slab, slab, slab, slab, slab, slab, slab,
             pltpu.VMEM((4, *block), jnp.bfloat16),
             pltpu.VMEM((3, *block), jnp.bfloat16),
             pltpu.VMEM((COARSE * TILE, DEPTH), jnp.bfloat16),
             pltpu.VMEM((DEPTH, FINE * TILE), jnp.bfloat16),
-            pltpu.VMEM((HALF, ROWS, TILE), jnp.bfloat16),
-            dma((5,)), dma, dma, dma, dma, dma, dma, dma, dma((4,)), dma, dma((4,)),
+            pltpu.VMEM((HALF, PIECE, TILE), jnp.bfloat16),
+            pltpu.VMEM((HALF, PIECE, TILE), jnp.bfloat16),
+            dma((5,)), dma, dma, dma, dma, dma, dma, dma, dma((4, 2)), dma, dma((4,)),
         ],
         compiler_params=pltpu.CompilerParams(
             collective_id=0, has_side_effects=True, vmem_limit_bytes=16 << 20
@@ -349,7 +375,7 @@
 
 def lag_tables():
     row = np.arange(DEPTH)
-    bin_number = 2 * (row // ROWS) + (row % ROWS) // 4 + 1.0
+    bin_number = 2 * (row % TILE // PIECE) + row // TILE + 1.0
     angle = np.pi / F * bin_number
     coarse = FINE * np.arange(COARSE) - LAGS // 2
     norm = 1.0 / math.sqrt(F * HOURS)

time: 35.5 us -> 35.3 us (level)
  no operation moved by 1% of the time
where the time goes in v7:
time: 35.3 us; the launch traced here: 35.2 us
  Pallas kernels  35.2 us (100%)
    pallas_call x1, Pallas kernels, fused(): pl.pallas_call(fused_kernel, out_shape=[jax.ShapeDtypeStruct((2, LAGS, TI...  32.5 us
    pallas_call x1, Pallas kernels, fused(): pl.pallas_call(finish_kernel, out_shape=jax.ShapeDtypeStruct((2, LAGS, TI...  2.68 us

profile of v7, /device:TPU:1, one launch (start us, length us, event | category | flops | bytes accessed | tf_op | source)
XLA Modules:
  0.0 35.2 jit_solution(5318467880232245210)
XLA Ops:
  0.0 32.5 %fused.1 = (f32[2,32,128,128]{3,2,1,0:T(8,128)S(1)}, bf16[32,2,4,4,128]{4,3,2,1,0:T(4,128)(2,1)S(1)}, f32[16,256]{1,0:T(8,128)S(1)}, f32[3,256,128]{2,1,0:T(8,12...) custom-call(bf16[256,96]{1,0:T(8,128)(2,1)} %bitcast.3, ...), custom_call_target="tpu_custom_call" | custom-call | tf_op jit(solution)/shard_map/fused/pallas_call | solution.py:320
  32.5 2.7 %finish.1 = f32[2,32,128,128]{3,2,1,0:T(8,128)} custom-call(bf16[32,2,4,4,128]{4,3,2,1,0:T(4,128)(2,1)S(1)} %get-tuple-element.12.last, f32[2,32,128,128]{3,2,1,0:T(8,128)S(1)} %get-tuple-element.13.partial, f32[16,256]{1,0:T(8,128)S(1)} %get-tuple-element.14.left_table, f32[3,256,128]{2,1,0:T(8,128)S(1)} %get-tuple-element.15.cosines, ...), custom_call_target="tpu_custom_call" | custom-call | tf_op jit(solution)/shard_map/finish/pallas_call | solution.py:360

commit v8 on v7

--- a/solution.py
+++ b/solution.py
@@ -62,15 +62,16 @@
 
 def lag_products(lhs, rhs, c, add):
     for n in range(2):
-        weights = rhs[:, 2 * n * TILE : (2 * n + 2) * TILE]
-        res = jnp.dot(lhs[c * TILE : (c + 2) * TILE, :], weights, preferred_element_type=jnp.float32)
+        weights = jnp.concatenate([part[:, 2 * n * TILE : (2 * n + 2) * TILE] for part in rhs], axis=0)
+        rotated = jnp.concatenate([part[c * TILE : (c + 2) * TILE, :] for part in lhs], axis=1)
+        res = jnp.dot(rotated, weights, preferred_element_type=jnp.float32)
         for dc in range(2):
             for dn in range(2):
                 lag = FINE * (c + dc) + 2 * n + dn
                 add(lag, res[dc * TILE : (dc + 1) * TILE, dn * TILE : (dn + 1) * TILE])
 
 
-def finish_kernel(last, partial, left_table, cosines, sines, swap, eye, out_hbm, stage, lhs, rhs, sems):
+def finish_kernel(last, lhs_late, rhs_late, partial, left_table, cosines, sines, swap, eye, out_hbm, stage, lhs, rhs, sems):
     copies = []
     for i in range(2):
         load_blocks(last, i, (0, 1), left_table, cosines, sines, swap, eye, lhs.at[i], rhs.at[i])
@@ -78,7 +79,7 @@
             def put(lag, value):
                 stage[i, lag] = partial[i, lag] + value
 
-            lag_products(lhs.at[i], rhs.at[i], c, put)
+            lag_products((lhs_late.at[i], lhs.at[i]), (rhs_late.at[i], rhs.at[i]), c, put)
             lags = pl.ds(FINE * c, 2 * FINE)
             copies.append(pltpu.make_async_copy(stage.at[i, lags], out_hbm.at[i, lags], sems.at[len(copies)]))
             copies[-1].start()
@@ -87,7 +88,7 @@
 
 
 def fused_kernel(
-    spec_hbm, bad_hbm, tile_hbm, left_hbm, right_hbm, out_ref, last, left_table, cosines, sines, swap, eye,
+    spec_hbm, bad_hbm, tile_hbm, left_hbm, right_hbm, out_ref, last, lhs_late, rhs_late, left_table, cosines, sines, swap, eye,
     spec, bad_ref, tile_ref, right_table, white, mine, mine_other, tiles_in, tiles, zb00, zb01, zb10, zb11, zb20, zb21, zb30, zb31, pack, got, lhs, rhs, other0, other1,
     sem_in, sem_a_send, sem_a_recv, sem_b_recv, sem_t_send, sem_t_recv, sem_t_local, sem_z_send, sem_z_recv,
     sem_p_send, sem_p_recv,
@@ -286,15 +287,25 @@
             def add(lag, value):
                 out_ref[i, lag] += value
 
-            bins = (lax.shift_right_logical(chunk, 1), 1 - lax.bitwise_and(chunk, 1))
+            bins = (0, 1 - chunk)
             load_blocks(part, i, bins, left_table, cosines, sines, swap, eye, lhs, rhs)
             for c in range(0, COARSE, 2):
-                lag_products(lhs, rhs, c, add)
+                lag_products((lhs,), (rhs,), c, add)
             return carry
 
         return lax.fori_loop(0, 2, one_tile, carry)
 
-    lax.fori_loop(0, 3, correlate, 0)
+    lax.fori_loop(0, 2, correlate, 0)
+
+    pltpu.make_async_copy(got.at[2], got.at[2], sem_p_recv.at[2]).wait()
+
+    def make_ready(i, carry):
+        load_blocks(
+            got.at[2], i, (1, 1), left_table, cosines, sines, swap, eye, lhs_late.at[i], rhs_late.at[i]
+        )
+        return carry
+
+    lax.fori_loop(0, 2, make_ready, 0)
 
     pltpu.make_async_copy(last, last, sem_p_recv.at[3]).wait()
     sent = white.at[pl.ds(0, PLANE - 1)]
@@ -322,6 +333,8 @@
         out_shape=[
             jax.ShapeDtypeStruct((2, LAGS, TILE, TILE), jnp.float32),
             jax.ShapeDtypeStruct(block, jnp.bfloat16),
+            jax.ShapeDtypeStruct((2, COARSE * TILE, DEPTH), jnp.bfloat16),
+            jax.ShapeDtypeStruct((2, DEPTH, FINE * TILE), jnp.bfloat16),
             jax.ShapeDtypeStruct((2 * COARSE, DEPTH), jnp.float32),
             jax.ShapeDtypeStruct(table, jnp.float32),
             jax.ShapeDtypeStruct(table, jnp.float32),
@@ -329,7 +342,7 @@
             jax.ShapeDtypeStruct((TILE, TILE), jnp.bfloat16),
         ],
         in_specs=[pl.BlockSpec(memory_space=pltpu.HBM)] * 5,
-        out_specs=[vmem] * 7,
+        out_specs=[vmem] * 9,
         scratch_shapes=[
             pltpu.VMEM((F * 4, SHARD), jnp.bfloat16),
             pltpu.VMEM((1, SHARD), jnp.int32),
@@ -360,7 +373,7 @@
     return pl.pallas_call(
         finish_kernel,
         out_shape=jax.ShapeDtypeStruct((2, LAGS, TILE, TILE), jnp.float32),
-        in_specs=[vmem] * 7,
+        in_specs=[vmem] * 9,
         out_specs=pl.BlockSpec(memory_space=pltpu.HBM),
         scratch_shapes=[
             pltpu.VMEM((2, LAGS, TILE, TILE), jnp.float32),
@@ -370,7 +383,7 @@
         ],
         compiler_params=pltpu.CompilerParams(vmem_limit_bytes=12 << 20),
         name="finish",
-    )(rest[0], partial, *rest[1:])
+    )(*rest[:3], partial, *rest[3:])
 
 
 def lag_tables():

time: 35.3 us -> 34.7 us (0.983)
  Pallas kernels: 35.2 us -> 34.6 us
    pallas_call x1, Pallas kernels: 32.5 us -> 31.7 us  [fused(): pl.pallas_call(fused_kernel, out_shape=[jax.ShapeDtypeStruct((2, LAGS, TI...]
where the time goes in v8:
time: 34.7 us; the launch traced here: 34.6 us
  Pallas kernels  34.6 us (100%)
    pallas_call x1, Pallas kernels, fused(): pl.pallas_call(fused_kernel, out_shape=[jax.ShapeDtypeStruct((2, LAGS, TI...  31.7 us
    pallas_call x1, Pallas kernels, fused(): pl.pallas_call(finish_kernel, out_shape=jax.ShapeDtypeStruct((2, LAGS, TI...  2.89 us

profile of v8, /device:TPU:1, one launch (start us, length us, event | category | flops | bytes accessed | tf_op | source)
XLA Modules:
  0.0 34.6 jit_solution(3779739643663933630)
XLA Ops:
  0.0 31.7 %fused.1 = (f32[2,32,128,128]{3,2,1,0:T(8,128)S(1)}, bf16[32,2,4,4,128]{4,3,2,1,0:T(4,128)(2,1)S(1)}, bf16[2,1024,256]{2,1,0:T(8,128)(2,1)S(1)}, bf16[2,256,512]...) custom-call(bf16[256,96]{1,0:T(8,128)(2,1)} %bitcast.3, ...), custom_call_target="tpu_custom_call" | custom-call | tf_op jit(solution)/shard_map/fused/pallas_call | solution.py:331
  31.7 2.9 %finish.1 = f32[2,32,128,128]{3,2,1,0:T(8,128)} custom-call(bf16[32,2,4,4,128]{4,3,2,1,0:T(4,128)(2,1)S(1)} %get-tuple-element.14.last, bf16[2,1024,256]{2,1,0:T(8,128)(2,1)S(1)} %get-tuple-element.15.lhs_late, bf16[2,256,512]{2,1,0:T(8,128)(2,1)S(1)} %get-tuple-element.16.rhs_late, f32[2,32,128,128]{3,2,1,0:T(8,128)S(1)} %get-tuple-element.17.partial, ...), custom_call_target="tpu_custom_call" | custom-call | tf_op jit(solution)/shard_map/finish/pallas_call | solution.py:373
